TPU v7x, 128 devices: a whole 4x4x4 slice. The times are simulated.
128 devices in a mesh: pop: 8 (over x, core), unit: 16 (over z, y).
Axes of the slice: x: 4, y: 4, z: 4, core: 2. Of those that a mesh axis runs over, the one named last changes fastest.
Arguments:
- states: bfloat16 [4, 4096, 1024], P(None, 'unit', 'pop'), may hold values from -6 to 6
- gate_inputs: bfloat16 [4, 3, 4096, 1024], P(None, None, 'unit', 'pop'), may hold values from -6 to 6
- actions: bfloat16 [4, 128, 1024], P(None, None, 'pop'), may hold values from -0.8984375 to 0.8984375
- final_grad: bfloat16 [4096, 1024], P('unit', 'pop'), may hold values from -6 to 6
- recur_weight: bfloat16 [4096, 3, 4096], P(None, None, 'unit'), may hold values from -0.09375 to 0.09375
- act_weight: bfloat16 [128, 3, 4096], P(None, None, 'unit'), may hold values from -0.5 to 0.5
- opp_first: bfloat16 [32, 4096, 4096], P('pop', None, 'unit'), may hold values from -0.09375 to 0.09375
- opp_second: bfloat16 [32, 128, 4096], P('pop'), may hold values from -0.09375 to 0.09375
- opponent: int32 [1024, 1], P('pop'), may hold values from 0 to 31; in each aligned block of 128 rows (0 to 127, 128 to 255, ...) at most 12 rows name the same one
Outputs:
- start_grad: bfloat16 [4096, 1024], P('unit', 'pop')
- act_weight_grad: float32 [128, 3, 4096], P(None, None, 'unit')
Inputs may be any that keep to these rules, and one draw needn't show every extreme that they name: In each aligned block of 128 rows (the rows of one index of pop) no opponent is named by more than 12 rows, a bound that some block reaches.
All inputs are finite; a program needn't handle non-finite values.
Results may differ from a plain program's by a relative error of at most 0.02.
Values may be sent and summed in bfloat16 or wider, within the bound.
A program may use at most 128 MiB of HBM per device.

v0:
```python
import jax
import jax.numpy as jnp
from jax import lax
from jax.sharding import PartitionSpec as P

CAP = 12


def gru_backward(gradient, pre_gates, latent):
    reset = jax.nn.sigmoid(pre_gates[0].astype(jnp.float32))
    cand_input = pre_gates[1].astype(jnp.float32)
    update = jax.nn.sigmoid(pre_gates[2].astype(jnp.float32) - 1.0)
    candidate = jnp.tanh(reset * cand_input)
    grad_cand = gradient * update * (1.0 - candidate * candidate)
    grad_reset = grad_cand * cand_input * reset * (1.0 - reset)
    grad_input = grad_cand * reset
    grad_update = gradient * (candidate - latent.astype(jnp.float32)) * update * (1.0 - update)
    direct = gradient * (1.0 - update)
    return (direct, jnp.stack([grad_reset, grad_input, grad_update]).astype(jnp.bfloat16))


def silu_slope(values):
    logistic = jax.nn.sigmoid(values)
    return logistic * (1.0 + values * (1.0 - logistic))


def hidden_slope(received, opp_first):
    members_here = received.shape[1]
    partial_sum = jnp.concatenate(
        [
            jnp.dot(opp_first[member], received[:, member, :], preferred_element_type=jnp.float32)
            for member in range(members_here)
        ],
        axis=1,
    )
    summed = lax.psum(partial_sum.astype(jnp.bfloat16), "unit").astype(jnp.float32)
    return silu_slope(summed)


def opponent_backward(slope, incoming, opp_first, opp_second):
    members_here = incoming.shape[1]
    slot_count = incoming.shape[2]
    upward = jnp.concatenate(
        [
            jnp.dot(
                opp_second[member].T, incoming[:, member, :], preferred_element_type=jnp.float32
            )
            for member in range(members_here)
        ],
        axis=1,
    )
    scaled = (upward * slope).astype(jnp.bfloat16)
    backward = jnp.concatenate(
        [
            jnp.dot(
                opp_first[member].T,
                scaled[:, member * slot_count : (member + 1) * slot_count],
                preferred_element_type=jnp.float32,
            )
            for member in range(members_here)
        ],
        axis=1,
    )
    return backward.astype(jnp.bfloat16).reshape(opp_first.shape[2], members_here, slot_count)


def body(
    states,
    gate_inputs,
    actions,
    final_grad,
    recur_weight,
    act_weight,
    opp_first,
    opp_second,
    opponent,
):
    step_count = states.shape[0]
    share = states.shape[1]
    row_count = states.shape[2]
    groups = lax.axis_size("pop")
    members_here = opp_first.shape[0]
    slot_count = groups * CAP
    population = members_here * groups
    chosen = opponent[:, 0]
    onehot = (chosen[:, None] == jnp.arange(population, dtype=jnp.int32)[None, :]).astype(jnp.int32)
    position = jnp.sum((jnp.cumsum(onehot, axis=0) - onehot) * onehot, axis=1)
    column = chosen % members_here * slot_count + chosen // members_here * CAP + position
    packing = (
        column[:, None] == jnp.arange(members_here * slot_count, dtype=jnp.int32)[None, :]
    ).astype(jnp.bfloat16)

    def pack_rows(values):
        packed = jnp.dot(values, packing, preferred_element_type=jnp.float32).astype(jnp.bfloat16)
        return packed.reshape(values.shape[0], members_here, slot_count)

    recur_flat = recur_weight.reshape(recur_weight.shape[0], -1)
    action_flat = act_weight.reshape(act_weight.shape[0], -1)
    gradient = final_grad.astype(jnp.float32)
    weight_grad = jnp.zeros(action_flat.shape, jnp.float32)
    for step in reversed(range(step_count)):
        direct, pre_grads = gru_backward(gradient, gate_inputs[step], states[step])
        flat_grads = pre_grads.reshape(-1, row_count)
        carried = lax.psum_scatter(
            jnp.dot(recur_flat, flat_grads, preferred_element_type=jnp.float32).astype(
                jnp.bfloat16
            ),
            "unit",
            scatter_dimension=0,
            tiled=True,
        ).astype(jnp.float32)
        action_grad = lax.psum(
            jnp.dot(action_flat, flat_grads, preferred_element_type=jnp.float32).astype(
                jnp.bfloat16
            ),
            "unit",
        ).astype(jnp.float32)
        weight_grad = weight_grad + jnp.dot(
            actions[step], flat_grads.T, preferred_element_type=jnp.float32
        )
        taken = actions[step].astype(jnp.float32)
        policy_grad = (action_grad * (1.0 - taken * taken)).astype(jnp.bfloat16)
        packed_grad = pack_rows(policy_grad)
        arrived_state, incoming = (
            lax.all_to_all(pack_rows(states[step]), "pop", split_axis=2, concat_axis=2, tiled=True),
            lax.all_to_all(packed_grad, "pop", split_axis=2, concat_axis=2, tiled=True),
        )
        slope = hidden_slope(arrived_state, opp_first)
        returned = lax.all_to_all(
            opponent_backward(slope, incoming, opp_first, opp_second),
            "pop",
            split_axis=2,
            concat_axis=2,
            tiled=True,
        )
        from_opponent = jnp.dot(
            returned.reshape(share, -1), packing.T, preferred_element_type=jnp.float32
        )
        gradient = direct + carried + from_opponent
    summed_weight = lax.psum(weight_grad.astype(jnp.bfloat16), "pop").astype(jnp.float32)
    return (gradient.astype(jnp.bfloat16), summed_weight.reshape(act_weight.shape))


def solution(mesh):
    placed = (
        P(None, "unit", "pop"),
        P(None, None, "unit", "pop"),
        P(None, None, "pop"),
        P("unit", "pop"),
        P(None, None, "unit"),
        P(None, None, "unit"),
        P("pop", None, "unit"),
        P("pop", None, None),
        P("pop", None),
    )
    return jax.shard_map(
        body,
        mesh=mesh,
        in_specs=placed,
        out_specs=(P("unit", "pop"), P(None, None, "unit")),
        check_vma=False,
    )
```

profile of v0, /device:TPU:1, one launch (start us, length us, event | category | flops | bytes accessed | tf_op | source)
XLA Modules:
  0.0 733.5 jit_solution(13641392170880029019)
XLA Ops:
  11.7 5.8 all-to-all-start.1
  23.5 4.8 all-to-all-start.4
  28.6 2.4 fusion.36
  30.9 2.4 fusion.37
  33.3 2.4 fusion.38
  35.6 2.4 fusion.39
  38.7 4.8 all-to-all-start.7
  43.5 1.6 fusion.381
  45.1 3.2 fusion.40
  48.4 3.3 fusion.41
  51.6 3.3 fusion.42
  54.9 3.3 fusion.43
  58.2 4.8 all-to-all-start.10
  63.8 3.2 fusion.44
  67.0 3.2 fusion.45
  70.3 3.3 fusion.46
  73.5 3.3 fusion.47
  78.4 2.4 fusion.48
  80.8 2.5 fusion.49
  83.3 2.4 fusion.50
  85.7 2.4 fusion.51
  88.2 3.1 pad_maximum_fusion
  91.6 3.0 pad_maximum_fusion.2
  97.0 65.1 %psum.63 = bf16[128,128]{0,1:T(8,128)(2,1)S(1)} all-reduce(bf16[128,128]{0,1:T(8,128)(2,1)S(1)} %fusion.205), channel_id=1, replica_groups=mesh['pop'=8,'unit'=16] {'unit'}, use_global_device_ids=true, to_apply=%region_1.2 | all-reduce | flops 16384 | bytes 65536 | tf_op jit(solution)/shard_map/psum | solution.py:112
  163.2 18.2 %all-to-all-start = ((bf16[128,4,96]{0,1,2:T(4,128)(2,1)}), bf16[128,4,96]{0,1,2:T(4,128)(2,1)S(1)}, u32[]{:S(2)}, u32[]{:S(2)}) async-start(bf16[128,4,96]{0,1,2:T(4,128)(2,1)} %copy.135), calls=%async_computation.1 | async-start | bytes 196608 | tf_op jit(solution)/shard_map/all_to_all | solution.py:126
  181.6 6.0 fusion.35
  199.0 1.7 convolution_bitcast_fusion.16
  205.4 72.5 %all-reduce.6.cloned.1.call-done = (bf16[4096,384]{0,1:T(8,128)(2,1)}, bf16[4096,384]{0,1:T(8,128)(2,1)}, bf16[4096,384]{0,1:T(8,128)(2,1)}, bf16[4096,384]{0,1:T(8,128)(2,1)}) async-done(((bf16[4096,384]{0,1:T(8,128)(2,1)}, bf16[4096,384]{0,1:T(8,128)(2,1)}, bf16[4096,384]{0,1:T(8,128)(2,1)}, bf16[4096,384]{0,1:T(8,128)(2,1)}), (bf16[4096,384]{0,1:T(8,128)(2,1)}, bf16[4096,384]{0,1:T(8,128)(2,1)}, ...) | async-done | bytes 12582928 | tf_op jit(solution)/shard_map/psum | solution.py:36
  277.9 4.4 fusion.6
  282.3 2.1 fusion.163
  284.4 2.1 fusion.175
  286.6 2.1 fusion.187
  288.7 2.1 fusion.199
  291.7 4.9 all-to-all-start.2
  296.9 5.7 all-to-all-done.2
  302.6 50.0 %reduce-scatter.5.cloned.1.call-done = bf16[256,128]{0,1:T(8,128)(2,1)} async-done(((bf16[4096,128]{0,1:T(8,128)(2,1)}), bf16[256,128]{0,1:T(8,128)(2,1)}) %reduce-scatter.5.cloned.1.call-update) | async-done | bytes 65552 | tf_op jit(solution)/shard_map/reduce_scatter | solution.py:104
  353.9 5.9 fusion.34
  360.1 58.3 %psum.65 = bf16[128,128]{0,1:T(8,128)(2,1)S(1)} all-reduce(bf16[128,128]{0,1:T(8,128)(2,1)S(1)} %fusion.204), channel_id=1, replica_groups=mesh['pop'=8,'unit'=16] {'unit'}, use_global_device_ids=true, to_apply=%region_6.7 | all-reduce | flops 16384 | bytes 65536 | tf_op jit(solution)/shard_map/psum | solution.py:112
  419.5 20.7 %all-to-all-start.3 = ((bf16[128,4,96]{0,1,2:T(4,128)(2,1)}), bf16[128,4,96]{0,1,2:T(4,128)(2,1)S(1)}, u32[]{:S(2)}, u32[]{:S(2)}) async-start(bf16[128,4,96]{0,1,2:T(4,128)(2,1)} %copy.154), calls=%async_computation.5 | async-start | bytes 196608 | tf_op jit(solution)/shard_map/all_to_all | solution.py:126
  440.3 4.7 all-to-all-done.3
  445.2 1.7 convolution_bitcast_fusion.12
  447.0 1.7 convolution_bitcast_fusion.13
  449.5 2.7 fusion.13
  455.4 4.1 all-to-all-start.5
  459.7 5.7 all-to-all-done.5
  466.7 5.9 fusion.33
  472.9 55.7 %psum.67 = bf16[128,128]{0,1:T(8,128)(2,1)S(1)} all-reduce(bf16[128,128]{0,1:T(8,128)(2,1)S(1)} %fusion.203), channel_id=1, replica_groups=mesh['pop'=8,'unit'=16] {'unit'}, use_global_device_ids=true, to_apply=%region_9.10 | all-reduce | flops 16384 | bytes 65536 | tf_op jit(solution)/shard_map/psum | solution.py:112
  529.7 18.1 %all-to-all-start.6 = ((bf16[128,4,96]{0,1,2:T(4,128)(2,1)}), bf16[128,4,96]{0,1,2:T(4,128)(2,1)S(1)}, u32[]{:S(2)}, u32[]{:S(2)}) async-start(bf16[128,4,96]{0,1,2:T(4,128)(2,1)} %copy.173), calls=%async_computation.9 | async-start | bytes 196608 | tf_op jit(solution)/shard_map/all_to_all | solution.py:126
  548.0 4.8 all-to-all-done.6
  553.0 1.7 convolution_bitcast_fusion.10
  554.7 1.7 convolution_bitcast_fusion.11
  557.2 2.7 fusion.20
  563.1 4.1 all-to-all-start.8
  567.7 5.4 all-to-all-done.8
  576.0 55.7 %psum.69 = bf16[128,128]{0,1:T(8,128)(2,1)S(1)} all-reduce(bf16[128,128]{0,1:T(8,128)(2,1)S(1)} %fusion.202), channel_id=1, replica_groups=mesh['pop'=8,'unit'=16] {'unit'}, use_global_device_ids=true, to_apply=%region_12.13 | all-reduce | flops 16384 | bytes 65536 | tf_op jit(solution)/shard_map/psum | solution.py:112
  632.7 18.1 %all-to-all-start.9 = ((bf16[128,4,96]{0,1,2:T(4,128)(2,1)}), bf16[128,4,96]{0,1,2:T(4,128)(2,1)S(1)}, u32[]{:S(2)}, u32[]{:S(2)}) async-start(bf16[128,4,96]{0,1,2:T(4,128)(2,1)} %copy.192), calls=%async_computation.13 | async-start | bytes 196608 | tf_op jit(solution)/shard_map/all_to_all | solution.py:126
  650.8 5.9 fusion.32
  656.9 1.7 convolution_bitcast_fusion.4
  658.7 1.7 convolution_bitcast_fusion.5
  661.2 2.7 fusion.27
  666.8 4.8 all-to-all-start.11
  671.6 1.7 reshape.206
  673.3 4.2 all-to-all-done.11
  677.5 47.0 %reduce-scatter.11.cloned.1.call-done = bf16[256,128]{0,1:T(8,128)(2,1)} async-done(((bf16[4096,128]{0,1:T(8,128)(2,1)}), bf16[256,128]{0,1:T(8,128)(2,1)}) %reduce-scatter.11.cloned.1.call-update) | async-done | bytes 65552 | tf_op jit(solution)/shard_map/reduce_scatter | solution.py:104
  (232 shorter events, 58.4 us)
Async XLA Ops:
  7.2 89.6 %copy-start = (bf16[128,3,256]{2,0,1:T(8,128)(2,1)S(1)}, bf16[128,3,256]{2,0,1:T(8,128)(2,1)}, u32[]{:S(2)}) copy-start(bf16[128,3,256]{2,0,1:T(8,128)(2,1)} %param.14) | copy-start | bytes 589828
  11.7 11.8 %all-to-all-start.1 = ((bf16[256,4,96]{0,1,2:T(4,128)(2,1)}), bf16[256,4,96]{0,1,2:T(4,128)(2,1)S(1)}, u32[]{:S(2)}, u32[]{:S(2)}) async-start(bf16[256,4,96]{0,1,2:T(4,128)(2,1)} %copy.140), calls=%async_computation.2 | async-start | bytes 393216 | tf_op jit(solution)/shard_map/all_to_all | solution.py:125
  23.5 14.5 %all-to-all-start.4 = ((bf16[256,4,96]{0,1,2:T(4,128)(2,1)}), bf16[256,4,96]{0,1,2:T(4,128)(2,1)S(1)}, u32[]{:S(2)}, u32[]{:S(2)}) async-start(bf16[256,4,96]{0,1,2:T(4,128)(2,1)} %copy.159), calls=%async_computation.6 | async-start | bytes 393216 | tf_op jit(solution)/shard_map/all_to_all | solution.py:125
  38.0 0.7 copy-start.16
  38.7 19.5 %all-to-all-start.7 = ((bf16[256,4,96]{0,1,2:T(4,128)(2,1)}), bf16[256,4,96]{0,1,2:T(4,128)(2,1)S(1)}, u32[]{:S(2)}, u32[]{:S(2)}) async-start(bf16[256,4,96]{0,1,2:T(4,128)(2,1)} %copy.178), calls=%async_computation.10 | async-start | bytes 393216 | tf_op jit(solution)/shard_map/all_to_all | solution.py:125
  58.2 18.7 %all-to-all-start.10 = ((bf16[256,4,96]{0,1,2:T(4,128)(2,1)}), bf16[256,4,96]{0,1,2:T(4,128)(2,1)}, u32[]{:S(2)}, u32[]{:S(2)}) async-start(bf16[256,4,96]{0,1,2:T(4,128)(2,1)} %copy.197), calls=%async_computation.14 | async-start | bytes 393216 | tf_op jit(solution)/shard_map/all_to_all | solution.py:125
  63.0 215.0 %all-reduce.6.cloned.1.call-start = ((), (), s32[]{:S(2)}) async-start(), calls=%async_computation.21 | async-start | bytes 25165824 | tf_op jit(solution)/shard_map/psum | solution.py:36
  80.8 7.3 copy-start.5
  80.8 7.3 copy-start.6
  80.8 7.3 copy-start.7
  80.8 7.3 copy-start.8
  88.1 3.1 copy-start.9
  88.1 3.1 copy-start.10
  88.1 3.1 copy-start.11
  88.1 3.4 copy-start.12
  94.6 1.1 copy-start.18
  94.6 1.5 copy-start.17
  94.6 1.7 copy-start.40
  94.6 1.8 copy-start.19
  95.9 91.8 %copy-start.33 = (bf16[1,1,256,128]{2,3,1,0:T(8,128)(2,1)}, bf16[1,1,256,128]{2,3,1,0:T(8,128)(2,1)S(1)}, u32[]{:S(2)}) copy-start(bf16[1,1,256,128]{2,3,1,0:T(8,128)(2,1)S(1)} %copy.215) | copy-start | bytes 196612
  163.2 35.7 %all-to-all-start = ((bf16[128,4,96]{0,1,2:T(4,128)(2,1)}), bf16[128,4,96]{0,1,2:T(4,128)(2,1)S(1)}, u32[]{:S(2)}, u32[]{:S(2)}) async-start(bf16[128,4,96]{0,1,2:T(4,128)(2,1)} %copy.135), calls=%async_computation.1 | async-start | bytes 196608 | tf_op jit(solution)/shard_map/all_to_all | solution.py:126
  181.4 171.2 %reduce-scatter.5.cloned.1.call-start = ((), (), s32[]{:S(2)}) async-start(), calls=%async_computation.16 | async-start | bytes 1114112 | tf_op jit(solution)/shard_map/reduce_scatter | solution.py:104
  198.8 3.5 copy-start.1
  286.5 10.1 %copy-start.20 = (bf16[4,128,128]{2,1,0:T(8,128)(2,1)S(1)}, bf16[4,128,128]{2,1,0:T(8,128)(2,1)}, u32[]{:S(2)}) copy-start(bf16[4,128,128]{2,1,0:T(8,128)(2,1)} %param.11) | copy-start | bytes 393220
  286.5 66.1 %copy-start.34 = (bf16[1,1,256,128]{2,3,1,0:T(8,128)(2,1)S(1)}, bf16[1,1,256,128]{2,3,1,0:T(8,128)(2,1)}, u32[]{:S(2)}) copy-start(bf16[1,1,256,128]{2,3,1,0:T(8,128)(2,1)} %copy-done.33) | copy-start | bytes 196612
  286.6 66.1 %copy-start.36 = (bf16[256,128]{0,1:T(8,128)(2,1)S(1)}, bf16[256,128]{0,1:T(8,128)(2,1)}, u32[]{:S(2)}) copy-start(bf16[256,128]{0,1:T(8,128)(2,1)} %copy-done.35) | copy-start | bytes 196612
  288.7 65.0 %copy-start.26 = (bf16[1,1,256,128]{2,3,1,0:T(8,128)(2,1)S(1)}, bf16[1,1,256,128]{2,3,1,0:T(8,128)(2,1)}, u32[]{:S(2)}) copy-start(bf16[1,1,256,128]{2,3,1,0:T(8,128)(2,1)} %copy.228) | copy-start | bytes 196612
  288.7 65.0 %copy-start.30 = (bf16[1,1,256,128]{2,3,1,0:T(8,128)(2,1)S(1)}, bf16[1,1,256,128]{2,3,1,0:T(8,128)(2,1)}, u32[]{:S(2)}) copy-start(bf16[1,1,256,128]{2,3,1,0:T(8,128)(2,1)} %copy.229) | copy-start | bytes 196612
  288.7 65.0 %copy-start.31 = (bf16[1,1,256,128]{2,3,1,0:T(8,128)(2,1)S(1)}, bf16[1,1,256,128]{2,3,1,0:T(8,128)(2,1)}, u32[]{:S(2)}) copy-start(bf16[1,1,256,128]{2,3,1,0:T(8,128)(2,1)} %copy.230) | copy-start | bytes 196612
  288.7 65.0 %copy-start.32 = (bf16[1,256,128]{1,2,0:T(8,128)(2,1)S(1)}, bf16[1,256,128]{1,2,0:T(8,128)(2,1)}, u32[]{:S(2)}) copy-start(bf16[1,256,128]{1,2,0:T(8,128)(2,1)} %copy.231) | copy-start | bytes 196612
  291.7 10.8 %all-to-all-start.2 = ((bf16[256,4,96]{0,1,2:T(4,128)(2,1)}), bf16[256,4,96]{0,1,2:T(4,128)(2,1)S(1)}, u32[]{:S(2)}, u32[]{:S(2)}) async-start(bf16[256,4,96]{0,1,2:T(4,128)(2,1)} %copy.145), calls=%async_computation.3 | async-start | bytes 393216 | tf_op jit(solution)/shard_map/all_to_all | solution.py:129
  296.7 168.8 %reduce-scatter.7.cloned.1.call-start = ((), (), s32[]{:S(2)}) async-start(), calls=%async_computation.17 | async-start | bytes 1114112 | tf_op jit(solution)/shard_map/reduce_scatter | solution.py:104
  353.9 64.5 %copy-start.39 = (bf16[1,128,128]{1,2,0:T(8,128)(2,1)S(1)}, bf16[1,128,128]{1,2,0:T(8,128)(2,1)}, u32[]{:S(2)}) copy-start(bf16[1,128,128]{1,2,0:T(8,128)(2,1)} %copy.232) | copy-start | bytes 98308
  419.5 25.6 %all-to-all-start.3 = ((bf16[128,4,96]{0,1,2:T(4,128)(2,1)}), bf16[128,4,96]{0,1,2:T(4,128)(2,1)S(1)}, u32[]{:S(2)}, u32[]{:S(2)}) async-start(bf16[128,4,96]{0,1,2:T(4,128)(2,1)} %copy.154), calls=%async_computation.5 | async-start | bytes 196608 | tf_op jit(solution)/shard_map/all_to_all | solution.py:126
  445.1 3.6 copy-start.2
  447.0 2.5 copy-start.15
  449.1 3.1 slice-start
  449.5 3.1 slice-start.1
  454.0 12.5 %copy-start.22 = (bf16[1,1,256,128]{2,3,1,0:T(8,128)(2,1)S(1)}, bf16[1,1,256,128]{2,3,1,0:T(8,128)(2,1)}, u32[]{:S(2)}) copy-start(bf16[1,1,256,128]{2,3,1,0:T(8,128)(2,1)} %copy.241) | copy-start | bytes 196612
  454.0 12.5 %copy-start.27 = (bf16[1,1,256,128]{2,3,1,0:T(8,128)(2,1)S(1)}, bf16[1,1,256,128]{2,3,1,0:T(8,128)(2,1)}, u32[]{:S(2)}) copy-start(bf16[1,1,256,128]{2,3,1,0:T(8,128)(2,1)} %copy.242) | copy-start | bytes 196612
  454.0 12.5 %copy-start.28 = (bf16[1,1,256,128]{2,3,1,0:T(8,128)(2,1)S(1)}, bf16[1,1,256,128]{2,3,1,0:T(8,128)(2,1)}, u32[]{:S(2)}) copy-start(bf16[1,1,256,128]{2,3,1,0:T(8,128)(2,1)} %copy.243) | copy-start | bytes 196612
  454.0 12.5 %copy-start.29 = (bf16[1,256,128]{1,2,0:T(8,128)(2,1)S(1)}, bf16[1,256,128]{1,2,0:T(8,128)(2,1)}, u32[]{:S(2)}) copy-start(bf16[1,256,128]{1,2,0:T(8,128)(2,1)} %copy.244) | copy-start | bytes 196612
  455.4 10.0 %all-to-all-start.5 = ((bf16[256,4,96]{0,1,2:T(4,128)(2,1)}), bf16[256,4,96]{0,1,2:T(4,128)(2,1)S(1)}, u32[]{:S(2)}, u32[]{:S(2)}) async-start(bf16[256,4,96]{0,1,2:T(4,128)(2,1)} %copy.164), calls=%async_computation.7 | async-start | bytes 393216 | tf_op jit(solution)/shard_map/all_to_all | solution.py:129
  459.5 113.7 %reduce-scatter.9.cloned.1.call-start = ((), (), s32[]{:S(2)}) async-start(), calls=%async_computation.18 | async-start | bytes 1114112 | tf_op jit(solution)/shard_map/reduce_scatter | solution.py:104
  466.7 61.9 %copy-start.38 = (bf16[1,128,128]{1,2,0:T(8,128)(2,1)S(1)}, bf16[1,128,128]{1,2,0:T(8,128)(2,1)}, u32[]{:S(2)}) copy-start(bf16[1,128,128]{1,2,0:T(8,128)(2,1)} %copy.245) | copy-start | bytes 98308
  529.7 23.1 %all-to-all-start.6 = ((bf16[128,4,96]{0,1,2:T(4,128)(2,1)}), bf16[128,4,96]{0,1,2:T(4,128)(2,1)S(1)}, u32[]{:S(2)}, u32[]{:S(2)}) async-start(bf16[128,4,96]{0,1,2:T(4,128)(2,1)} %copy.173), calls=%async_computation.9 | async-start | bytes 196608 | tf_op jit(solution)/shard_map/all_to_all | solution.py:126
  552.8 3.6 copy-start.3
  554.7 2.5 copy-start.14
  556.8 3.1 slice-start.2
  557.2 3.1 slice-start.3
  561.7 12.6 %copy-start.21 = (bf16[1,1,256,128]{2,3,1,0:T(8,128)(2,1)S(1)}, bf16[1,1,256,128]{2,3,1,0:T(8,128)(2,1)}, u32[]{:S(2)}) copy-start(bf16[1,1,256,128]{2,3,1,0:T(8,128)(2,1)} %copy.254) | copy-start | bytes 196612
  561.7 12.6 %copy-start.23 = (bf16[1,1,256,128]{2,3,1,0:T(8,128)(2,1)S(1)}, bf16[1,1,256,128]{2,3,1,0:T(8,128)(2,1)}, u32[]{:S(2)}) copy-start(bf16[1,1,256,128]{2,3,1,0:T(8,128)(2,1)} %copy.255) | copy-start | bytes 196612
  561.7 12.6 %copy-start.24 = (bf16[1,1,256,128]{2,3,1,0:T(8,128)(2,1)S(1)}, bf16[1,1,256,128]{2,3,1,0:T(8,128)(2,1)}, u32[]{:S(2)}) copy-start(bf16[1,1,256,128]{2,3,1,0:T(8,128)(2,1)} %copy.256) | copy-start | bytes 196612
  561.7 12.5 %copy-start.25 = (bf16[1,256,128]{1,2,0:T(8,128)(2,1)S(1)}, bf16[1,256,128]{1,2,0:T(8,128)(2,1)}, u32[]{:S(2)}) copy-start(bf16[1,256,128]{1,2,0:T(8,128)(2,1)} %copy.257) | copy-start | bytes 196612
  562.2 69.4 %copy-start.37 = (bf16[1,128,128]{1,2,0:T(8,128)(2,1)S(1)}, bf16[1,128,128]{1,2,0:T(8,128)(2,1)}, u32[]{:S(2)}) copy-start(bf16[1,128,128]{1,2,0:T(8,128)(2,1)} %copy.258) | copy-start | bytes 98308
  563.1 10.0 %all-to-all-start.8 = ((bf16[256,4,96]{0,1,2:T(4,128)(2,1)}), bf16[256,4,96]{0,1,2:T(4,128)(2,1)S(1)}, u32[]{:S(2)}, u32[]{:S(2)}) async-start(bf16[256,4,96]{0,1,2:T(4,128)(2,1)} %copy.183), calls=%async_computation.11 | async-start | bytes 393216 | tf_op jit(solution)/shard_map/all_to_all | solution.py:129
  567.2 104.4 %all-reduce.4.cloned.1.call-start = ((), (), s32[]{:S(2)}) async-start(), calls=%async_computation.20 | async-start | bytes 393216 | tf_op jit(solution)/shard_map/psum | solution.py:140
  632.7 24.0 %all-to-all-start.9 = ((bf16[128,4,96]{0,1,2:T(4,128)(2,1)}), bf16[128,4,96]{0,1,2:T(4,128)(2,1)S(1)}, u32[]{:S(2)}, u32[]{:S(2)}) async-start(bf16[128,4,96]{0,1,2:T(4,128)(2,1)} %copy.192), calls=%async_computation.13 | async-start | bytes 196608 | tf_op jit(solution)/shard_map/all_to_all | solution.py:126
  650.8 73.7 %reduce-scatter.11.cloned.1.call-start = ((), (), s32[]{:S(2)}) async-start(), calls=%async_computation.19 | async-start | bytes 1114112 | tf_op jit(solution)/shard_map/reduce_scatter | solution.py:104
  656.7 3.7 copy-start.4
  658.6 2.5 copy-start.13
  660.4 3.5 slice-start.4
  661.2 2.8 slice-start.5
  666.8 10.7 %all-to-all-start.11 = ((bf16[256,4,96]{0,1,2:T(4,128)(2,1)}), bf16[256,4,96]{0,1,2:T(4,128)(2,1)S(1)}, u32[]{:S(2)}, u32[]{:S(2)}) async-start(bf16[256,4,96]{0,1,2:T(4,128)(2,1)} %copy.202), calls=%async_computation.15 | async-start | bytes 393216 | tf_op jit(solution)/shard_map/all_to_all | solution.py:129
  (1 other events, 0.6 us)
Sparse Core Ops, SparseCore 0:
  94.7 183.1 all-reduce.5
  281.5 71.0 reduce-scatter.4
  360.2 72.3 reduce-scatter.6
  473.0 66.2 reduce-scatter.8
  576.1 52.2 all-reduce.3
  656.9 67.6 reduce-scatter.10
where the time goes:
time: 742 us; the launch traced here: 733 us
  blocking collectives  235 us (32%)
  waiting for transfers between devices  200 us (27%)
  starting transfers between devices  114 us (15%)
  matrix products  113 us (15%)
  local copies, waits for them, and re-layouts  31.5 us (4%)
  other arithmetic  23.6 us (3%)
  between operations  15.5 us (2%)
    psum x4, blocking collectives, body(): lax.psum(jnp.dot(action_flat, flat_grads, preferred_element_type=jnp.floa...  235 us
    reduce_scatter x4, waiting for transfers between devices, body(): lax.psum_scatter(jnp.dot(recur_flat, flat_grads, preferred_element_type=j...  97.1 us
    all_to_all x4, starting transfers between devices, body(): lax.all_to_all(packed_grad, 'pop', split_axis=2, concat_axis=2, tiled=True)  75.1 us
    psum x1, waiting for transfers between devices, hidden_slope(): lax.psum(partial_sum.astype(jnp.bfloat16), 'unit').astype(jnp.float32)  72.5 us
    dot_general x16, matrix products, hidden_slope(): jnp.dot(opp_first[member], received[:, member, :], preferred_element_type...  45 us
    dot_general x4, matrix products, body(): jnp.dot(recur_flat, flat_grads, preferred_element_type=jnp.float32)  23.8 us
    all_to_all x4, waiting for transfers between devices, body(): lax.all_to_all(opponent_backward(slope, incoming, opp_first, opp_second),...  21 us
    all_to_all x4, starting transfers between devices, body(): lax.all_to_all(pack_rows(states[step]), 'pop', split_axis=2, concat_axis=...  20.2 us
  transfers between devices with their start and end apart: 18, of which 9 were waited for; matrix products, arithmetic and copies ran while one was open for 17% of the time, Pallas kernels for 0%

commit v1 on v0

v1 whole, which is shorter than its diff:
```python
import functools
import types

import jax
import jax.numpy as jnp
from jax import lax
from jax.experimental import pallas as pl
from jax.experimental.pallas import tpu as pltpu
from jax.sharding import PartitionSpec as P

MESH = pl.DeviceIdType.MESH
F32 = jnp.float32
BF16 = jnp.bfloat16
PAIR = 48
RING = 4


def mm(a, b):
    return jnp.dot(a, b, preferred_element_type=F32)


def mm_nt(a, b):
    return lax.dot_general(a, b, (((1,), (1,)), ((), ())), preferred_element_type=F32)


def silu_slope(values):
    logistic = jax.nn.sigmoid(values)
    return logistic * (1.0 + values * (1.0 - logistic))


class Wire:
    def __init__(self, send_sems, recv_sems):
        self.send_sems = send_sems
        self.recv_sems = recv_sems
        self.count = 0

    def send(self, source, target, device):
        number = self.count
        self.count += 1
        copy = pltpu.make_async_remote_copy(
            src_ref=source,
            dst_ref=target,
            send_sem=self.send_sems.at[number],
            recv_sem=self.recv_sems.at[number],
            device_id=device,
            device_id_type=MESH,
        )
        copy.start()
        return copy, number, device

    def arrived(self, sent, landing):
        pltpu.make_async_remote_copy(
            src_ref=landing,
            dst_ref=landing,
            send_sem=self.send_sems.at[sent[1]],
            recv_sem=self.recv_sems.at[sent[1]],
            device_id=sent[2],
            device_id_type=MESH,
        ).wait_recv()


def wait_sends(sent):
    for entry in sent:
        entry[0].wait_send()


class Scatter:
    def __init__(self, wire, held, lo, hi, first, second, one, two, three, four, rest):
        self.wire, self.held, self.lo, self.hi = wire, held, lo, hi
        self.first, self.second = first, second
        self.one, self.two, self.three, self.four, self.rest = one, two, three, four, rest
        self.width = hi - lo

    def part(self, index, a, b):
        return self.held.at[index, a:b, :, self.lo : self.hi]

    def line(self, index, a, b):
        return self.rest.at[index, a:b, 0 : self.width]

    def stage1(self):
        w, (me, plus, minus) = self.wire, self.first
        up, down, far = (me + 1) % RING, (me + 3) % RING, (me + 2) % RING
        self.s1 = [
            w.send(self.part(far, 0, 2), self.one.at[0], plus),
            w.send(self.part(far, 2, 4), self.one.at[1], minus),
            w.send(self.part(up, 2, 4), self.two.at[0, 2:4], plus),
            w.send(self.part(down, 0, 2), self.two.at[1, 0:2], minus),
        ]

    def stage2(self):
        w, (me, plus, minus) = self.wire, self.first
        up, down = (me + 1) % RING, (me + 3) % RING
        lo, hi = self.lo, self.hi
        self.s2 = []
        for side, block, base, device in ((0, up, 0, plus), (1, down, 2, minus)):
            w.arrived(self.s1[side], self.one.at[side])

            def add(i, carry, side=side, block=block, base=base):
                total = self.held[block, base + i, :, lo:hi].astype(F32)
                total = total + self.one[side, i].astype(F32)
                self.held[block, base + i, :, lo:hi] = total.astype(BF16)
                return carry

            lax.fori_loop(0, 2, add, 0)
            self.s2.append(
                w.send(
                    self.part(block, base, base + 2), self.two.at[side, base : base + 2], device
                )
            )

    def stage3(self):
        w, me = self.wire, self.first[0]
        at, plus, minus = self.second
        lo, hi = self.lo, self.hi
        w.arrived(self.s1[2], self.two.at[0, 2:4])
        w.arrived(self.s1[3], self.two.at[1, 0:2])
        w.arrived(self.s2[0], self.two.at[0, 0:2])
        w.arrived(self.s2[1], self.two.at[1, 2:4])

        def add(i, carry):
            total = self.held[me, i, :, lo:hi].astype(F32) + self.two[0, i].astype(F32)
            total = total + self.two[1, i].astype(F32)
            self.rest[i, :, 0 : self.width] = total.astype(BF16)
            return carry

        lax.fori_loop(0, RING, add, 0)
        up, down, far = (at + 1) % RING, (at + 3) % RING, (at + 2) % RING
        self.s3 = [
            w.send(self.line(far, 0, 64), self.three.at[0], plus),
            w.send(self.line(far, 64, 128), self.three.at[1], minus),
            w.send(self.line(up, 64, 128), self.four.at[0, 64:128], plus),
            w.send(self.line(down, 0, 64), self.four.at[1, 0:64], minus),
        ]

    def stage4(self):
        w = self.wire
        at, plus, minus = self.second
        up, down = (at + 1) % RING, (at + 3) % RING
        self.s4 = []
        for side, block, base, device in ((0, up, 0, plus), (1, down, 64, minus)):
            w.arrived(self.s3[side], self.three.at[side])
            total = self.rest[block, base : base + 64, 0 : self.width].astype(F32)
            total = total + self.three[side].astype(F32)
            self.rest[block, base : base + 64, 0 : self.width] = total.astype(BF16)
            self.s4.append(
                w.send(
                    self.line(block, base, base + 64), self.four.at[side, base : base + 64], device
                )
            )

    def landed(self):
        w = self.wire
        w.arrived(self.s3[2], self.four.at[0, 64:128])
        w.arrived(self.s3[3], self.four.at[1, 0:64])
        w.arrived(self.s4[0], self.four.at[0, 0:64])
        w.arrived(self.s4[1], self.four.at[1, 64:128])
        wait_sends(self.s1 + self.s2 + self.s3 + self.s4)

    def result(self, a, b):
        total = self.rest[self.second[0], :, a:b].astype(F32) + self.four[0, :, a:b].astype(F32)
        return total + self.four[1, :, a:b].astype(F32)


class Gather:
    def __init__(self, wire, held, rows, first, second):
        self.wire, self.held, self.rows = wire, held, rows
        self.first, self.second = first, second

    def stage1(self):
        f, (at, plus, minus) = self.first[0], self.second
        own = self.held.at[f, at]
        self.a1 = [self.wire.send(own, own, plus), self.wire.send(own, own, minus)]

    def stage2(self):
        f, (at, plus, minus) = self.first[0], self.second
        half = self.rows // 2
        below, above = (at + 3) % RING, (at + 1) % RING
        self.wire.arrived(self.a1[0], self.held.at[f, below])
        low = self.held.at[f, below, 0:half]
        first = self.wire.send(low, low, plus)
        self.wire.arrived(self.a1[1], self.held.at[f, above])
        high = self.held.at[f, above, half : 2 * half]
        self.a2 = [first, self.wire.send(high, high, minus)]

    def stage3(self):
        f, plus, minus = self.first
        at = self.second[0]
        half = self.rows // 2
        far = (at + 2) % RING
        self.wire.arrived(self.a2[0], self.held.at[f, far, 0:half])
        self.wire.arrived(self.a2[1], self.held.at[f, far, half : 2 * half])
        line = self.held.at[f]
        self.a3 = [self.wire.send(line, line, plus), self.wire.send(line, line, minus)]

    def stage4(self):
        f, plus, minus = self.first
        below, above = (f + 3) % RING, (f + 1) % RING
        self.wire.arrived(self.a3[0], self.held.at[below])
        low = self.held.at[below, 0:2]
        first = self.wire.send(low, low, plus)
        self.wire.arrived(self.a3[1], self.held.at[above])
        high = self.held.at[above, 2:4]
        self.a4 = [first, self.wire.send(high, high, minus)]

    def landed(self):
        far = (self.first[0] + 2) % RING
        self.wire.arrived(self.a4[0], self.held.at[far, 0:2])
        self.wire.arrived(self.a4[1], self.held.at[far, 2:4])
        wait_sends(self.a1 + self.a2 + self.a3 + self.a4)


def kernel(
    steps,
    cap,
    groups,
    members,
    blocks,
    states,
    gates,
    actions,
    final_grad,
    act_w,
    opp_row,
    opp_col,
    recur_hbm,
    first_hbm,
    second_hbm,
    start_out,
    weight_out,
    *scratch,
):
    shapes = scratch_shapes(steps, cap, groups, members, blocks)
    s = types.SimpleNamespace(**jax.tree.unflatten(jax.tree.structure(shapes), scratch))
    rows = 128
    half = cap // 2
    last = steps - 1
    pair_rows = groups * PAIR
    p = lax.axis_index("pop")
    u = lax.axis_index("unit")
    z, y = u // RING, u % RING

    def at_unit(zz, yy):
        return (p, (zz % RING) * RING + yy % RING)

    z_ring = (z, at_unit(z + 1, y), at_unit(z + 3, y))
    y_ring = (y, at_unit(z, y + 1), at_unit(z, y + 3))
    z_peers = [at_unit(z + k, y) for k in (1, 2, 3)]
    y_peers = [at_unit(z, y + k) for k in (1, 2, 3)]
    pop_peers = [((p + k) % groups, u) for k in range(1, groups)]
    barrier = pltpu.get_barrier_semaphore()
    for device in z_peers + y_peers + pop_peers:
        pl.semaphore_signal(barrier, inc=1, device_id=device, device_id_type=MESH)

    loads = [
        pltpu.make_async_copy(first_hbm, s.first, s.load_sems.at[0]),
        pltpu.make_async_copy(recur_hbm, s.recur, s.load_sems.at[1]),
        pltpu.make_async_copy(second_hbm, s.second, s.load_sems.at[2]),
    ]
    for load in loads:
        load.start()
    wire = Wire(s.send_sems, s.recv_sems)

    def keys(chosen, axis):
        shape = (8, rows) if axis == 1 else (rows, 8)
        group_of = (chosen // members).astype(F32)
        index = lax.broadcasted_iota(jnp.int32, shape, 1 - axis).astype(F32)
        onehot = jnp.where(group_of == index, 1.0, 0.0)
        a = lax.broadcasted_iota(jnp.int32, (rows, rows), 0)
        b = lax.broadcasted_iota(jnp.int32, (rows, rows), 1)
        if axis == 1:
            rank = mm(onehot.astype(BF16), jnp.where(a < b, 1.0, 0.0).astype(BF16))
        else:
            rank = mm(jnp.where(b < a, 1.0, 0.0).astype(BF16), onehot.astype(BF16))
        return jnp.sum(onehot * (rank + index * PAIR), axis=1 - axis, keepdims=True)

    key_row = keys(opp_row[...], 1)
    key_col = keys(opp_col[...], 0)
    slot = lax.broadcasted_iota(jnp.int32, (pair_rows, rows), 0).astype(F32)
    s.pack[...] = jnp.where(slot == key_row, 1.0, 0.0).astype(BF16)
    slot = lax.broadcasted_iota(jnp.int32, (rows, pair_rows), 1).astype(F32)
    s.unpack[...] = jnp.where(slot == key_col, 1.0, 0.0).astype(BF16)
    ident = (opp_col[...] % members + 1).astype(F32)
    ident = jnp.broadcast_to(ident, (rows, 128)).astype(BF16)
    ident = mm(s.pack[...], ident).astype(BF16)
    packed = mm_nt(s.pack[...], states[last]).astype(BF16)
    for g in range(groups):
        s.out_late[g, :, 0:256] = packed[g * PAIR : (g + 1) * PAIR]
        s.out_late[g, :, 256:384] = ident[g * PAIR : (g + 1) * PAIR]

    pl.semaphore_wait(barrier, len(z_peers + y_peers + pop_peers))

    def exchange(source, target):
        sent = [
            wire.send(source.at[(p + k) % groups], target.at[p], device)
            for k, device in zip(range(1, groups), pop_peers)
        ]
        target[p] = source[p]
        return sent

    def exchanged(sent, target):
        for k, entry in zip(range(1, groups), sent):
            wire.arrived(entry, target.at[(p + groups - k) % groups])

    late = exchange(s.out_late, s.in_late)
    for t in range(last):
        packed = mm_nt(s.pack[...], states[t]).astype(BF16)
        for g in range(groups):
            s.out_early[g, t] = packed[g * PAIR : (g + 1) * PAIR]
    early = exchange(s.out_early, s.in_early)

    def factors(t):
        reset = jax.nn.sigmoid(gates[t, 0].astype(F32))
        cand_in = gates[t, 1].astype(F32)
        update = jax.nn.sigmoid(gates[t, 2].astype(F32) - 1.0)
        candidate = jnp.tanh(reset * cand_in)
        e = update * (1.0 - candidate * candidate)
        rest = 1.0 - update
        s.factor[t, 0] = e * cand_in * reset * (1.0 - reset)
        s.factor[t, 1] = e * reset
        s.factor[t, 2] = (candidate - states[t].astype(F32)) * update * rest
        s.factor[t, 3] = rest
        taken = actions[t].astype(F32)
        s.bound[t] = 1.0 - taken * taken

    factors(last)
    s.grad[...] = final_grad[...].astype(F32)

    def begin(t):
        for q in range(3):
            s.pre[q] = (s.grad[...] * s.factor[t, q]).astype(BF16)
        part = mm(act_w[0], s.pre[0]) + mm(act_w[1], s.pre[1]) + mm(act_w[2], s.pre[2])
        s.act_own[t, 0] = part.astype(BF16)
        return [
            wire.send(s.act_own.at[t, 0], s.act_in.at[t, 0, i], device)
            for i, device in enumerate(z_peers)
        ]

    def act_sum(t, stage, sent):
        for i, entry in enumerate(sent):
            wire.arrived(entry, s.act_in.at[t, stage, i])
        total = s.act_own[t, stage].astype(F32) + s.act_in[t, stage, 0].astype(F32)
        total = total + s.act_in[t, stage, 1].astype(F32)
        return total + s.act_in[t, stage, 2].astype(F32)

    def act_second(t, sent):
        s.act_own[t, 1] = act_sum(t, 0, sent).astype(BF16)
        return [
            wire.send(s.act_own.at[t, 1], s.act_in.at[t, 1, i], device)
            for i, device in enumerate(y_peers)
        ]

    def dispatch(t, sent):
        policy = (act_sum(t, 1, sent) * s.bound[t]).astype(BF16)
        packed = mm_nt(s.pack[...], policy).astype(BF16)
        for g in range(groups):
            s.policy_out[t, g] = packed[g * PAIR : (g + 1) * PAIR]
        return exchange(s.policy_out.at[t], s.policy_in.at[t])

    def collect(t, sent):
        exchanged(sent, s.policy_in.at[t])
        arrived = s.policy_in[t].reshape(pair_rows, 128)
        policy = mm(s.choose[...], arrived).astype(BF16)
        for m in range(members):
            s.policy[:, m * 128 : (m + 1) * 128] = policy * s.mask[m, :, 0:128]

    def store_blocks(b, total, lo):
        hi = lo + total.shape[1]
        s.held_a[b // RING, b % RING, :, lo:hi] = total[0:128]
        s.held_b[b % RING, b // RING, :, lo:hi] = total[128:256]

    def carried_part():
        def two(i, carry):
            at = pl.ds(pl.multiple_of(i * 512, 512), 512)
            total = mm(s.recur[0, at, :], s.pre[0]) + mm(s.recur[1, at, :], s.pre[1])
            total = (total + mm(s.recur[2, at, :], s.pre[2])).astype(BF16)
            store_blocks(2 * i, total[0:256], 0)
            store_blocks(2 * i + 1, total[256:512], 0)
            return carry

        lax.fori_loop(0, blocks // 2, two, 0)

    def weight_part(t, start):
        for q in range(3):
            share = mm_nt(actions[t], s.pre[q])
            at = slice(q * 256, (q + 1) * 256)
            if start:
                s.weight[:, at] = share
            else:
                s.weight[:, at] += share

    def latents(t):
        if t == last:
            arrived = s.in_late[:, :, 0:256].reshape(pair_rows, 256)
        else:
            arrived = s.in_early[:, t].reshape(pair_rows, 256)
        chosen = mm(s.choose[...], arrived).T
        for m in range(members):
            s.latent[m] = jnp.where(s.names[0:1] == m + 1, chosen, 0.0).astype(BF16)

    def hidden_part(t):
        latents(t)

        def two(i, carry):
            at = pl.ds(pl.multiple_of(i * 512, 512), 512)
            total = mm(s.first[0, at, :], s.latent[0])
            for m in range(1, members):
                total = total + mm(s.first[m, at, :], s.latent[m])
            total = total.astype(BF16)
            store_blocks(2 * i, total[0:256], 128)
            store_blocks(2 * i + 1, total[256:512], 128)
            return carry

        lax.fori_loop(0, blocks // 2, two, 0)

    def scatters(which, lo, hi):
        one, two = s.sums[which]
        return [
            Scatter(wire, s.held_a, lo, hi, z_ring, y_ring, *one, s.rest_a),
            Scatter(wire, s.held_b, lo, hi, y_ring, z_ring, *two, s.rest_b),
        ]

    def slopes(t, pair, lo):
        hidden = jnp.concatenate([one.result(lo, lo + cap) for one in pair], axis=0)
        slope = silu_slope(hidden).T.astype(BF16)
        s.slope_a[t % 2, z, y] = slope[0:half]
        s.slope_b[t % 2, y, z] = slope[half:cap]
        made = [
            Gather(wire, s.slope_a.at[t % 2], half, z_ring, y_ring),
            Gather(wire, s.slope_b.at[t % 2], half, y_ring, z_ring),
        ]
        for one in made:
            one.stage1()
        return made

    def backward(t):
        def one(b, carry):
            at = pl.ds(pl.multiple_of(b * 256, 256), 256)
            upward = mm(s.policy[:, 0:128], s.second[0, :, at])
            for m in range(1, members):
                upward = upward + mm(s.policy[:, m * 128 : (m + 1) * 128], s.second[m, :, at])
            low = upward[0:half] * s.slope_a[t % 2, b // RING, b % RING].astype(F32)
            high = upward[half:cap] * s.slope_b[t % 2, b % RING, b // RING].astype(F32)
            s.scaled[0:half, at] = low.astype(BF16)
            s.scaled[half:cap, at] = high.astype(BF16)
            return carry

        lax.fori_loop(0, blocks, one, 0)
        s.back[...] = jnp.zeros_like(s.back)

        def member(m, carry):
            s.back[...] += s.mask[m].astype(F32) * mm(s.scaled[...], s.first[m])
            return carry

        lax.fori_loop(0, members, member, 0)
        packed = mm(s.spread[...], s.back[...].astype(BF16)).astype(BF16)
        for g in range(groups):
            s.return_out[t, g] = packed[g * PAIR : (g + 1) * PAIR]
        return exchange(s.return_out.at[t], s.return_in.at[t])

    def finish(t, sent, pair):
        exchanged(sent, s.return_in.at[t])
        own = mm(s.unpack[...], s.return_in[t].reshape(pair_rows, 256)).T
        direct = s.grad[...] * s.factor[t, 3]
        s.grad[0:128] = direct[0:128] + pair[0].result(0, 128) + own[0:128]
        s.grad[128:256] = direct[128:256] + pair[1].result(0, 128) + own[128:256]

    sends = []
    act = begin(last)

    exchanged(late, s.in_late)
    names_in = s.in_late[:, :, 256:384].reshape(pair_rows, 128)
    lane = lax.broadcasted_iota(jnp.int32, (8, 128), 1)
    picker = jnp.where(lane == 0, 1.0, 0.0).astype(BF16)
    names_row = mm_nt(picker, names_in)
    held_row = jnp.where(names_row > 0.5, 1.0, 0.0)
    a = lax.broadcasted_iota(jnp.int32, (pair_rows, pair_rows), 0)
    b = lax.broadcasted_iota(jnp.int32, (pair_rows, pair_rows), 1)
    place_row = mm(held_row.astype(BF16), jnp.where(a < b, 1.0, 0.0).astype(BF16))
    spot = lax.broadcasted_iota(jnp.int32, (cap, pair_rows), 0).astype(F32)
    chosen = jnp.where(spot == place_row[0:1], held_row[0:1], 0.0).astype(BF16)
    s.choose[...] = chosen
    held_col = jnp.where(names_in.astype(F32) > 0.5, 1.0, 0.0)
    place_col = mm(jnp.where(b < a, 1.0, 0.0).astype(BF16), held_col.astype(BF16))
    spot = lax.broadcasted_iota(jnp.int32, (pair_rows, cap), 1).astype(F32)
    chosen_t = jnp.where(spot == place_col[:, 0:1], held_col[:, 0:1], 0.0)
    s.spread[...] = chosen_t.astype(BF16)
    s.names[...] = mm(names_row.astype(BF16), s.spread[...])
    slot_name = mm(s.choose[...], names_in)
    for m in range(members):
        mask = jnp.where(jnp.abs(slot_name[:, 0:1] - (m + 1)) < 0.5, 1.0, 0.0)
        s.mask[m] = jnp.broadcast_to(mask, (cap, 256)).astype(BF16)

    loads[0].wait()
    hidden_part(last)
    opening = scatters(steps, 128, 128 + cap)
    for one in opening:
        one.stage1()
    act2 = act_second(last, act)
    loads[1].wait()
    carried_part()
    for one in opening:
        one.stage2()
    sends += act + act2
    out = dispatch(last, act2)
    weight_part(last, True)
    for one in opening:
        one.stage3()
    for t in range(last):
        factors(t)
    exchanged(early, s.in_early)
    for one in opening:
        one.stage4()
    loads[2].wait()
    collect(last, out)
    for one in opening:
        one.landed()
    gather = slopes(last, opening, 0)
    hidden_part(last - 1)
    pair = scatters(last, 0, 128 + cap)
    for one in pair:
        one.stage1()
    for one in gather:
        one.stage2()
    for one in pair:
        one.stage2()
    for one in gather:
        one.stage3()
    for one in pair:
        one.stage3()
    for one in gather:
        one.stage4()
    for one in pair:
        one.stage4()
    for one in gather:
        one.landed()
    sends += late + early + out

    for t in range(last, -1, -1):
        if t < last:
            act = begin(t)
            if t > 0:
                pair = scatters(t, 0, 128 + cap)
            else:
                pair = scatters(t, 0, 128)
            carried_part()
            for one in pair:
                one.stage1()
            for one in gather:
                one.stage3()
            act2 = act_second(t, act)
            weight_part(t, False)
            for one in pair:
                one.stage2()
            for one in gather:
                one.stage4()
            if t == 0:
                pieces = [
                    s.weight[k * 16 : (k + 1) * 16].astype(BF16) for k in range(groups)
                ]
                for k in range(groups):
                    s.share_out[k] = pieces[k]
                shares = exchange(s.share_out, s.share_in)
            out = dispatch(t, act2)
            for one in pair:
                one.stage3()
            sends += act + act2 + out
            collect(t, out)
            for one in pair:
                one.stage4()
            if t == 0:
                exchanged(shares, s.share_in)
                total = s.share_in[0].astype(F32)
                for k in range(1, groups):
                    total = total + s.share_in[k].astype(F32)
                s.share_all[p] = total.astype(BF16)
                whole = [
                    wire.send(s.share_all.at[p], s.share_all.at[p], device)
                    for device in pop_peers
                ]
                sends += shares + whole
            for one in gather:
                one.landed()
        back = backward(t)
        sends += back
        for one in pair:
            one.landed()
        if t > 0:
            gather = slopes(t - 1, pair, 128)
            if t > 1:
                hidden_part(t - 2)
            for one in gather:
                one.stage2()
        else:
            exchanged(whole, s.share_all)
            for k in range(groups):
                weight_out[k * 16 : (k + 1) * 16] = s.share_all[k].astype(F32)
        finish(t, back, pair)
    start_out[...] = s.grad[...].astype(BF16)
    wait_sends(sends)


def sum_bufs(width):
    def four():
        return (
            pltpu.VMEM((2, 2, 128, width), BF16),
            pltpu.VMEM((2, RING, 128, width), BF16),
            pltpu.VMEM((2, 64, width), BF16),
            pltpu.VMEM((2, 128, width), BF16),
        )

    return four(), four()


def scratch_shapes(steps, cap, groups, members, blocks):
    half = cap // 2
    v = pltpu.VMEM
    shapes = dict(
        first=v((members, blocks * 256, 256), BF16),
        recur=v((3, blocks * 256, 256), BF16),
        second=v((members, 128, blocks * 256), BF16),
        pack=v((groups * PAIR, 128), BF16),
        unpack=v((128, groups * PAIR), BF16),
        choose=v((cap, groups * PAIR), BF16),
        spread=v((groups * PAIR, cap), BF16),
        mask=v((members, cap, 256), BF16),
        out_late=v((groups, PAIR, 384), BF16),
        in_late=v((groups, PAIR, 384), BF16),
        out_early=v((groups, steps - 1, PAIR, 256), BF16),
        in_early=v((groups, steps - 1, PAIR, 256), BF16),
        factor=v((steps, 4, 256, 128), F32),
        bound=v((steps, 128, 128), F32),
        grad=v((256, 128), F32),
        pre=v((3, 256, 128), BF16),
        act_own=v((steps, 2, 128, 128), BF16),
        act_in=v((steps, 2, 3, 128, 128), BF16),
        policy_out=v((steps, groups, PAIR, 128), BF16),
        policy_in=v((steps, groups, PAIR, 128), BF16),
        policy=v((cap, members * 128), BF16),
        latent=v((members, 256, cap), BF16),
        names=v((8, cap), F32),
        scaled=v((cap, blocks * 256), BF16),
        weight=v((128, 768), F32),
        share_out=v((groups, 16, 768), BF16),
        share_in=v((groups, 16, 768), BF16),
        share_all=v((groups, 16, 768), BF16),
        back=v((cap, 256), F32),
        return_out=v((steps, groups, PAIR, 256), BF16),
        return_in=v((steps, groups, PAIR, 256), BF16),
        held_a=v((RING, RING, 128, 128 + cap), BF16),
        held_b=v((RING, RING, 128, 128 + cap), BF16),
        rest_a=v((RING, 128, 128 + cap), BF16),
        rest_b=v((RING, 128, 128 + cap), BF16),
        slope_a=v((2, RING, RING, half, 256), BF16),
        slope_b=v((2, RING, RING, half, 256), BF16),
    )
    shapes.update(sums=[sum_bufs(128 + cap if t > 0 else 128) for t in range(steps)] + [sum_bufs(cap)])
    copies = 4 * (groups - 1) + (steps + 1) * 24 + steps * (16 + 6 + 2 * (groups - 1))
    shapes.update(send_sems=pltpu.SemaphoreType.DMA((copies,)))
    shapes.update(recv_sems=pltpu.SemaphoreType.DMA((copies,)))
    shapes.update(load_sems=pltpu.SemaphoreType.DMA((3,)))
    return shapes


def call(cap, groups, blocks, name, collective_id):
    def run(states, gates, actions, final_grad, act_w, opp_row, opp_col, recur, first, second):
        steps, members = states.shape[0], first.shape[0]
        vmem = pl.BlockSpec(memory_space=pltpu.VMEM)
        hbm = pl.BlockSpec(memory_space=pl.ANY)
        return pl.pallas_call(
            functools.partial(kernel, steps, cap, groups, members, blocks),
            out_shape=(
                jax.ShapeDtypeStruct((256, 128), BF16),
                jax.ShapeDtypeStruct((128, 768), F32),
            ),
            in_specs=[vmem] * 7 + [hbm] * 3,
            out_specs=(vmem, vmem),
            scratch_shapes=jax.tree.leaves(scratch_shapes(steps, cap, groups, members, blocks)),
            compiler_params=pltpu.CompilerParams(
                collective_id=collective_id, has_side_effects=True, vmem_limit_bytes=62 << 20
            ),
            name=name,
        )(states, gates, actions, final_grad, act_w, opp_row, opp_col, recur, first, second)

    return run


def body(
    states,
    gate_inputs,
    actions,
    final_grad,
    recur_weight,
    act_weight,
    opp_first,
    opp_second,
    opponent,
):
    groups = lax.axis_size("pop")
    blocks = lax.axis_size("unit")
    cap = groups * PAIR
    recur = jnp.transpose(recur_weight, (1, 0, 2))
    act_w = jnp.transpose(act_weight, (1, 0, 2))
    start, weight = call(cap, groups, blocks, "steps_back", 0)(
        states,
        gate_inputs,
        actions,
        final_grad,
        act_w,
        opponent.reshape(1, -1),
        opponent,
        recur,
        opp_first,
        opp_second,
    )
    return start, weight.reshape(act_weight.shape)


def solution(mesh):
    placed = (
        P(None, "unit", "pop"),
        P(None, None, "unit", "pop"),
        P(None, None, "pop"),
        P("unit", "pop"),
        P(None, None, "unit"),
        P(None, None, "unit"),
        P("pop", None, "unit"),
        P("pop", None, None),
        P("pop", None),
    )
    return jax.shard_map(
        body,
        mesh=mesh,
        in_specs=placed,
        out_specs=(P("unit", "pop"), P(None, None, "unit")),
        check_vma=False,
    )
```

time: 742 us -> 264 us (0.36); the launches traced: 733 us -> 264 us
  Pallas kernels: 0 us -> 258 us
  blocking collectives: 235 us -> 0 us
  waiting for transfers between devices: 200 us -> 0 us
  starting transfers between devices: 114 us -> 0 us
  matrix products: 113 us -> 0 us
  local copies, waits for them, and re-layouts: 31.5 us -> 4.93 us
  other arithmetic: 23.6 us -> 0 us
  between operations: 15.5 us -> 0.65 us
    pallas_call x0 -> x1, Pallas kernels: none -> 258 us  [run(): pl.pallas_call(functools.partial(kernel, steps, cap, groups, members, blo...]
    psum x4 -> x0, blocking collectives: 235 us -> none  [body(): lax.psum(jnp.dot(action_flat, flat_grads, preferred_element_type=jnp.floa...]
    dot_general x72 -> x0, matrix products: 113 us -> none  [the longest x16 45 us: hidden_slope(): jnp.dot(opp_first[member], received[:, member, :], preferred_element_type...]
    all_to_all x12 -> x0, starting transfers between devices: 113 us -> none  [the longest x4 75.1 us: body(): lax.all_to_all(packed_grad, 'pop', split_axis=2, concat_axis=2, tiled=True)]
    reduce_scatter x4 -> x0, waiting for transfers between devices: 97.1 us -> none  [body(): lax.psum_scatter(jnp.dot(recur_flat, flat_grads, preferred_element_type=j...]
    psum x2 -> x0, waiting for transfers between devices: 72.6 us -> none  [the longest x1 72.5 us: hidden_slope(): lax.psum(partial_sum.astype(jnp.bfloat16), 'unit').astype(jnp.float32)]
    all_to_all x12 -> x0, waiting for transfers between devices: 30.6 us -> none  [the longest x4 21 us: body(): lax.all_to_all(opponent_backward(slope, incoming, opp_first, opp_second),...]
    convert_element_type x5 -> x0, other arithmetic: 13.3 us -> none  [the longest x4 12.5 us: opponent_backward(): scaled = (upward * slope).astype(jnp.bfloat16)]
  transfers between devices with their start and end apart: 18 -> 0, of which waited for: 9 -> 0; matrix products, arithmetic and copies ran while one was open for 17% -> 0% of each run, Pallas kernels for 0% -> 0%
where the time goes in v1:
time: 264 us
  Pallas kernels  258 us (98%)
  local copies, waits for them, and re-layouts  4.93 us (2%)
    pallas_call x1, Pallas kernels, run(): pl.pallas_call(functools.partial(kernel, steps, cap, groups, members, blo...  258 us

profile of v1, /device:TPU:1, one launch (start us, length us, event | category | flops | bytes accessed | tf_op | source)
XLA Modules:
  0.0 263.6 jit_solution(6631217313301542433)
XLA Ops:
  0.6 1.4 copy.13.opp_col
  2.0 258.0 %steps_back.1 = (bf16[256,128]{1,0:T(8,128)(2,1)}, f32[128,768]{1,0:T(8,128)}) custom-call(bf16[4,256,128]{2,1,0:T(8,128)(2,1)} %states.1, bf16[4,3,256,128]{3,2,1,0:T(8,128)(2,1)} %gates.1, bf16[4,128,128]{2,1,0:T(8,128)(2,1)} %actions.1, bf16[256,128]{1,0:T(8,128)(2,1)} %final_grad.1, bf16[3,128,256]{2,1,0:T(8,128)(2,1)} %bitcast.6, s32[1,128]{1,0:T(1,128)} %bitcast.7, ...), custom_call_target="tpu_custom_call" | custom-call | tf_op jit(solution)/shard_map/steps_back/pallas_call | solution.py:669
  260.1 1.2 copy.14
  261.2 0.9 copy.15
  262.1 1.5 copy.17

commit v2 on v1

--- a/solution.py
+++ b/solution.py
@@ -12,6 +12,7 @@
 F32 = jnp.float32
 BF16 = jnp.bfloat16
 PAIR = 48
+FEW = 256
 RING = 4
 
 
@@ -77,12 +78,18 @@
     def line(self, index, a, b):
         return self.rest.at[index, a:b, 0 : self.width]
 
+    def stage0(self):
+        w, (me, plus, minus) = self.wire, self.first
+        far = (me + 2) % RING
+        self.s0 = [
+            w.send(self.part(far, 0, 2), self.one.at[0], plus),
+            w.send(self.part(far, 2, 4), self.one.at[1], minus),
+        ]
+
     def stage1(self):
         w, (me, plus, minus) = self.wire, self.first
-        up, down, far = (me + 1) % RING, (me + 3) % RING, (me + 2) % RING
+        up, down = (me + 1) % RING, (me + 3) % RING
         self.s1 = [
-            w.send(self.part(far, 0, 2), self.one.at[0], plus),
-            w.send(self.part(far, 2, 4), self.one.at[1], minus),
             w.send(self.part(up, 2, 4), self.two.at[0, 2:4], plus),
             w.send(self.part(down, 0, 2), self.two.at[1, 0:2], minus),
         ]
@@ -93,7 +100,7 @@
         lo, hi = self.lo, self.hi
         self.s2 = []
         for side, block, base, device in ((0, up, 0, plus), (1, down, 2, minus)):
-            w.arrived(self.s1[side], self.one.at[side])
+            w.arrived(self.s0[side], self.one.at[side])
 
             def add(i, carry, side=side, block=block, base=base):
                 total = self.held[block, base + i, :, lo:hi].astype(F32)
@@ -112,8 +119,8 @@
         w, me = self.wire, self.first[0]
         at, plus, minus = self.second
         lo, hi = self.lo, self.hi
-        w.arrived(self.s1[2], self.two.at[0, 2:4])
-        w.arrived(self.s1[3], self.two.at[1, 0:2])
+        w.arrived(self.s1[0], self.two.at[0, 2:4])
+        w.arrived(self.s1[1], self.two.at[1, 0:2])
         w.arrived(self.s2[0], self.two.at[0, 0:2])
         w.arrived(self.s2[1], self.two.at[1, 2:4])
 
@@ -154,7 +161,7 @@
         w.arrived(self.s3[3], self.four.at[1, 0:64])
         w.arrived(self.s4[0], self.four.at[0, 0:64])
         w.arrived(self.s4[1], self.four.at[1, 64:128])
-        wait_sends(self.s1 + self.s2 + self.s3 + self.s4)
+        wait_sends(self.s0 + self.s1 + self.s2 + self.s3 + self.s4)
 
     def result(self, a, b):
         total = self.rest[self.second[0], :, a:b].astype(F32) + self.four[0, :, a:b].astype(F32)
@@ -212,6 +219,7 @@
 def kernel(
     steps,
     cap,
+    deep,
     groups,
     members,
     blocks,
@@ -229,7 +237,7 @@
     weight_out,
     *scratch,
 ):
-    shapes = scratch_shapes(steps, cap, groups, members, blocks)
+    shapes = scratch_shapes(steps, cap, deep, groups, members, blocks)
     s = types.SimpleNamespace(**jax.tree.unflatten(jax.tree.structure(shapes), scratch))
     rows = 128
     half = cap // 2
@@ -327,8 +335,8 @@
 
     def begin(t):
         for q in range(3):
-            s.pre[q] = (s.grad[...] * s.factor[t, q]).astype(BF16)
-        part = mm(act_w[0], s.pre[0]) + mm(act_w[1], s.pre[1]) + mm(act_w[2], s.pre[2])
+            s.pre[q * 256 : (q + 1) * 256] = (s.grad[...] * s.factor[t, q]).astype(BF16)
+        part = mm(jnp.concatenate([act_w[q] for q in range(3)], axis=1), s.pre[...])
         s.act_own[t, 0] = part.astype(BF16)
         return [
             wire.send(s.act_own.at[t, 0], s.act_in.at[t, 0, i], device)
@@ -368,25 +376,23 @@
         s.held_a[b // RING, b % RING, :, lo:hi] = total[0:128]
         s.held_b[b % RING, b // RING, :, lo:hi] = total[128:256]
 
-    def carried_part():
+    def carried_part(lo):
         def two(i, carry):
             at = pl.ds(pl.multiple_of(i * 512, 512), 512)
-            total = mm(s.recur[0, at, :], s.pre[0]) + mm(s.recur[1, at, :], s.pre[1])
-            total = (total + mm(s.recur[2, at, :], s.pre[2])).astype(BF16)
-            store_blocks(2 * i, total[0:256], 0)
-            store_blocks(2 * i + 1, total[256:512], 0)
+            wide = jnp.concatenate([s.recur[q, at, :] for q in range(3)], axis=1)
+            total = mm(wide, s.pre[...]).astype(BF16)
+            store_blocks(2 * i, total[0:256], lo)
+            store_blocks(2 * i + 1, total[256:512], lo)
             return carry
 
         lax.fori_loop(0, blocks // 2, two, 0)
 
     def weight_part(t, start):
-        for q in range(3):
-            share = mm_nt(actions[t], s.pre[q])
-            at = slice(q * 256, (q + 1) * 256)
-            if start:
-                s.weight[:, at] = share
-            else:
-                s.weight[:, at] += share
+        share = mm_nt(actions[t], s.pre[...])
+        if start:
+            s.weight[...] = share
+        else:
+            s.weight[...] += share
 
     def latents(t):
         if t == last:
@@ -395,28 +401,26 @@
             arrived = s.in_early[:, t].reshape(pair_rows, 256)
         chosen = mm(s.choose[...], arrived).T
         for m in range(members):
-            s.latent[m] = jnp.where(s.names[0:1] == m + 1, chosen, 0.0).astype(BF16)
-
-    def hidden_part(t):
+            s.latent[m * 256 : (m + 1) * 256] = jnp.where(s.names[0:1] == m + 1, chosen, 0.0).astype(BF16)
+
+    def hidden_part(t, lo):
         latents(t)
 
         def two(i, carry):
             at = pl.ds(pl.multiple_of(i * 512, 512), 512)
-            total = mm(s.first[0, at, :], s.latent[0])
-            for m in range(1, members):
-                total = total + mm(s.first[m, at, :], s.latent[m])
-            total = total.astype(BF16)
-            store_blocks(2 * i, total[0:256], 128)
-            store_blocks(2 * i + 1, total[256:512], 128)
+            wide = jnp.concatenate([s.first[m, at, :] for m in range(members)], axis=1)
+            total = mm(wide, s.latent[...]).astype(BF16)
+            store_blocks(2 * i, total[0:256], lo)
+            store_blocks(2 * i + 1, total[256:512], lo)
             return carry
 
         lax.fori_loop(0, blocks // 2, two, 0)
 
-    def scatters(which, lo, hi):
-        one, two = s.sums[which]
+    def scatters(bufs, rest, lo, hi):
+        one, two = bufs
         return [
-            Scatter(wire, s.held_a, lo, hi, z_ring, y_ring, *one, s.rest_a),
-            Scatter(wire, s.held_b, lo, hi, y_ring, z_ring, *two, s.rest_b),
+            Scatter(wire, s.held_a, lo, hi, z_ring, y_ring, *one, rest[0]),
+            Scatter(wire, s.held_b, lo, hi, y_ring, z_ring, *two, rest[1]),
         ]
 
     def slopes(t, pair, lo):
@@ -424,27 +428,38 @@
         slope = silu_slope(hidden).T.astype(BF16)
         s.slope_a[t % 2, z, y] = slope[0:half]
         s.slope_b[t % 2, y, z] = slope[half:cap]
-        made = [
+        return [
             Gather(wire, s.slope_a.at[t % 2], half, z_ring, y_ring),
             Gather(wire, s.slope_b.at[t % 2], half, y_ring, z_ring),
         ]
-        for one in made:
-            one.stage1()
-        return made
-
-    def backward(t):
-        def one(b, carry):
-            at = pl.ds(pl.multiple_of(b * 256, 256), 256)
-            upward = mm(s.policy[:, 0:128], s.second[0, :, at])
-            for m in range(1, members):
-                upward = upward + mm(s.policy[:, m * 128 : (m + 1) * 128], s.second[m, :, at])
-            low = upward[0:half] * s.slope_a[t % 2, b // RING, b % RING].astype(F32)
-            high = upward[half:cap] * s.slope_b[t % 2, b % RING, b // RING].astype(F32)
-            s.scaled[0:half, at] = low.astype(BF16)
-            s.scaled[half:cap, at] = high.astype(BF16)
+
+    def upward_part(i):
+        at = pl.ds(pl.multiple_of(i * 1024, 1024), 1024)
+        return mm(s.policy[...], s.second[:, at])
+
+    def upward_ahead():
+        def four(i, carry):
+            s.upward[:, pl.ds(pl.multiple_of(i * 1024, 1024), 1024)] = upward_part(i)
             return carry
 
-        lax.fori_loop(0, blocks, one, 0)
+        lax.fori_loop(0, blocks // RING, four, 0)
+
+    def backward(t, ahead):
+        def four(i, carry):
+            if ahead:
+                upward = s.upward[:, pl.ds(pl.multiple_of(i * 1024, 1024), 1024)]
+            else:
+                upward = upward_part(i)
+            for j in range(RING):
+                at = pl.ds(pl.multiple_of(i * 1024 + j * 256, 256), 256)
+                here = slice(j * 256, (j + 1) * 256)
+                low = upward[0:half, here] * s.slope_a[t % 2, i, j].astype(F32)
+                high = upward[half:cap, here] * s.slope_b[t % 2, j, i].astype(F32)
+                s.scaled[0:half, at] = low.astype(BF16)
+                s.scaled[half:cap, at] = high.astype(BF16)
+            return carry
+
+        lax.fori_loop(0, blocks // RING, four, 0)
         s.back[...] = jnp.zeros_like(s.back)
 
         def member(m, carry):
@@ -457,12 +472,12 @@
             s.return_out[t, g] = packed[g * PAIR : (g + 1) * PAIR]
         return exchange(s.return_out.at[t], s.return_in.at[t])
 
-    def finish(t, sent, pair):
+    def finish(t, sent, pair, lo):
         exchanged(sent, s.return_in.at[t])
         own = mm(s.unpack[...], s.return_in[t].reshape(pair_rows, 256)).T
         direct = s.grad[...] * s.factor[t, 3]
-        s.grad[0:128] = direct[0:128] + pair[0].result(0, 128) + own[0:128]
-        s.grad[128:256] = direct[128:256] + pair[1].result(0, 128) + own[128:256]
+        s.grad[0:128] = direct[0:128] + pair[0].result(lo, lo + 128) + own[0:128]
+        s.grad[128:256] = direct[128:256] + pair[1].result(lo, lo + 128) + own[128:256]
 
     sends = []
     act = begin(last)
@@ -490,111 +505,190 @@
         mask = jnp.where(jnp.abs(slot_name[:, 0:1] - (m + 1)) < 0.5, 1.0, 0.0)
         s.mask[m] = jnp.broadcast_to(mask, (cap, 256)).astype(BF16)
 
+    def first_shares():
+        for k in range(groups):
+            s.share_out[k] = s.weight[k * 16 : (k + 1) * 16].astype(BF16)
+        return exchange(s.share_out, s.share_in)
+
+    def second_shares(shares):
+        exchanged(shares, s.share_in)
+        total = s.share_in[0].astype(F32)
+        for k in range(1, groups):
+            total = total + s.share_in[k].astype(F32)
+        s.share_all[p] = total.astype(BF16)
+        whole = [wire.send(s.share_all.at[p], s.share_all.at[p], device) for device in pop_peers]
+        sends.extend(shares + whole)
+        return whole
+
+    def last_shares(whole):
+        exchanged(whole, s.share_all)
+        for k in range(groups):
+            for q in range(3):
+                weight_out[q, k * 16 : (k + 1) * 16] = s.share_all[k, :, q * 256 : (q + 1) * 256].astype(F32)
+
+    def stage(pair, *numbers):
+        for number in numbers:
+            for one in pair:
+                if number == 0:
+                    one.stage0()
+                else:
+                    (one.stage1, one.stage2, one.stage3, one.stage4, one.landed)[number - 1]()
+
     loads[0].wait()
-    hidden_part(last)
-    opening = scatters(steps, 128, 128 + cap)
-    for one in opening:
-        one.stage1()
-    act2 = act_second(last, act)
-    loads[1].wait()
-    carried_part()
-    for one in opening:
-        one.stage2()
-    sends += act + act2
-    out = dispatch(last, act2)
-    weight_part(last, True)
-    for one in opening:
-        one.stage3()
-    for t in range(last):
-        factors(t)
-    exchanged(early, s.in_early)
-    for one in opening:
-        one.stage4()
-    loads[2].wait()
-    collect(last, out)
-    for one in opening:
-        one.landed()
-    gather = slopes(last, opening, 0)
-    hidden_part(last - 1)
-    pair = scatters(last, 0, 128 + cap)
-    for one in pair:
-        one.stage1()
-    for one in gather:
-        one.stage2()
-    for one in pair:
-        one.stage2()
-    for one in gather:
-        one.stage3()
-    for one in pair:
-        one.stage3()
-    for one in gather:
-        one.stage4()
-    for one in pair:
-        one.stage4()
-    for one in gather:
-        one.landed()
-    sends += late + early + out
-
-    for t in range(last, -1, -1):
-        if t < last:
-            act = begin(t)
+    if deep:
+        early_lo, carried_lo, late_lo = 0, cap, cap + 128
+        hidden_part(last, early_lo)
+        opening = scatters(s.sums[steps], s.rests[1], early_lo, early_lo + cap)
+        stage(opening, 0, 1)
+        act2 = act_second(last, act)
+        exchanged(early, s.in_early)
+        hidden_part(last - 1, late_lo)
+        second = scatters(s.sums[steps + 1], s.rests[0], late_lo, late_lo + cap)
+        stage(opening, 2)
+        stage(second, 0)
+        loads[1].wait()
+        carried_part(carried_lo)
+        pair = scatters(s.sums[last], s.rests[2], carried_lo, late_lo)
+        stage(opening, 3)
+        stage(second, 1)
+        out = dispatch(last, act2)
+        weight_part(last, True)
+        stage(opening, 4)
+        stage(second, 2)
+        stage(pair, 0, 1)
+        stage(opening, 5)
+        gather = slopes(last, opening, 0)
+        stage(gather, 1)
+        stage(second, 3)
+        stage(pair, 2)
+        hidden_part(last - 2, early_lo)
+        later = scatters(s.sums[steps + 2], s.rests[1], early_lo, early_lo + cap)
+        stage(gather, 2)
+        stage(second, 4)
+        stage(pair, 3)
+        loads[2].wait()
+        collect(last, out)
+        upward_ahead()
+        stage(gather, 3)
+        stage(second, 5)
+        following = slopes(last - 1, second, 0)
+        stage(pair, 4)
+        for t in range(last):
+            factors(t)
+        stage(gather, 4)
+        stage(following, 1)
+        stage(later, 0, 1)
+        stage(gather, 5)
+        stage(following, 2)
+        sends += act + act2 + late + early + out
+        back = backward(last, True)
+        stage(later, 2)
+        stage(following, 3)
+        hidden_part(0, late_lo)
+        for t in range(last, -1, -1):
+            if t < last:
+                gather = following
+                act = begin(t)
+                carried_part(carried_lo)
+                pair = scatters(s.sums[t], s.rests[2], carried_lo, late_lo)
+                if t > 0:
+                    stage(later, 3)
+                act2 = act_second(t, act)
+                stage(pair, 0, 1)
+                if t > 0:
+                    stage(later, 4)
+                stage(gather, 4)
+                weight_part(t, False)
+                if t == 0:
+                    shares = first_shares()
+                out = dispatch(t, act2)
+                sends += act + act2 + out
+                stage(pair, 2)
+                if t > 0:
+                    stage(later, 5)
+                    following = slopes(t - 1, later, 0)
+                    stage(following, 1)
+                if t == last - 1:
+                    later = scatters(s.sums[steps + 3], s.rests[0], late_lo, late_lo + cap)
+                    stage(later, 0, 1)
+                collect(t, out)
+                stage(pair, 3)
+                if t == 0:
+                    whole = second_shares(shares)
+                if t > 0:
+                    stage(following, 2)
+                stage(gather, 5)
+                back = backward(t, False)
+                stage(pair, 4)
+                if t == last - 1:
+                    stage(later, 2)
+                if t > 0:
+                    stage(following, 3)
+            sends += back
+            stage(pair, 5)
+            if t == 0:
+                last_shares(whole)
+            finish(t, back, pair, 0)
+    else:
+        hidden_part(last, 128)
+        opening = scatters(s.sums[steps], s.rests[0], 128, 128 + cap)
+        stage(opening, 0, 1)
+        act2 = act_second(last, act)
+        loads[1].wait()
+        carried_part(0)
+        stage(opening, 2)
+        out = dispatch(last, act2)
+        weight_part(last, True)
+        stage(opening, 3)
+        for t in range(last):
+            factors(t)
+        exchanged(early, s.in_early)
+        stage(opening, 4)
+        loads[2].wait()
+        collect(last, out)
+        stage(opening, 5)
+        gather = slopes(last, opening, 0)
+        stage(gather, 1)
+        hidden_part(last - 1, 128)
+        pair = scatters(s.sums[last], s.rests[0], 0, 128 + cap)
+        stage(pair, 0)
+        for number in range(1, 5):
+            stage(pair, number)
+            stage(gather, number + 1)
+        sends += act + act2 + late + early + out
+        for t in range(last, -1, -1):
+            if t < last:
+                act = begin(t)
+                pair = scatters(s.sums[t], s.rests[0], 0, 128 + cap if t > 0 else 128)
+                carried_part(0)
+                stage(pair, 0, 1)
+                stage(gather, 3)
+                act2 = act_second(t, act)
+                weight_part(t, False)
+                stage(pair, 2)
+                stage(gather, 4)
+                if t == 0:
+                    shares = first_shares()
+                out = dispatch(t, act2)
+                stage(pair, 3)
+                sends += act + act2 + out
+                collect(t, out)
+                stage(pair, 4)
+                if t == 0:
+                    whole = second_shares(shares)
+                stage(gather, 5)
+            back = backward(t, False)
+            sends += back
+            stage(pair, 5)
             if t > 0:
-                pair = scatters(t, 0, 128 + cap)
+                gather = slopes(t - 1, pair, 128)
+                stage(gather, 1)
+                if t > 1:
+                    hidden_part(t - 2, 128)
+                stage(gather, 2)
             else:
-                pair = scatters(t, 0, 128)
-            carried_part()
-            for one in pair:
-                one.stage1()
-            for one in gather:
-                one.stage3()
-            act2 = act_second(t, act)
-            weight_part(t, False)
-            for one in pair:
-                one.stage2()
-            for one in gather:
-                one.stage4()
-            if t == 0:
-                pieces = [
-                    s.weight[k * 16 : (k + 1) * 16].astype(BF16) for k in range(groups)
-                ]
-                for k in range(groups):
-                    s.share_out[k] = pieces[k]
-                shares = exchange(s.share_out, s.share_in)
-            out = dispatch(t, act2)
-            for one in pair:
-                one.stage3()
-            sends += act + act2 + out
-            collect(t, out)
-            for one in pair:
-                one.stage4()
-            if t == 0:
-                exchanged(shares, s.share_in)
-                total = s.share_in[0].astype(F32)
-                for k in range(1, groups):
-                    total = total + s.share_in[k].astype(F32)
-                s.share_all[p] = total.astype(BF16)
-                whole = [
-                    wire.send(s.share_all.at[p], s.share_all.at[p], device)
-                    for device in pop_peers
-                ]
-                sends += shares + whole
-            for one in gather:
-                one.landed()
-        back = backward(t)
-        sends += back
-        for one in pair:
-            one.landed()
-        if t > 0:
-            gather = slopes(t - 1, pair, 128)
-            if t > 1:
-                hidden_part(t - 2)
-            for one in gather:
-                one.stage2()
-        else:
-            exchanged(whole, s.share_all)
-            for k in range(groups):
-                weight_out[k * 16 : (k + 1) * 16] = s.share_all[k].astype(F32)
-        finish(t, back, pair)
+                last_shares(whole)
+            finish(t, back, pair, 0)
     start_out[...] = s.grad[...].astype(BF16)
     wait_sends(sends)
 
@@ -611,13 +705,14 @@
     return four(), four()
 
 
-def scratch_shapes(steps, cap, groups, members, blocks):
+def scratch_shapes(steps, cap, deep, groups, members, blocks):
     half = cap // 2
+    held = 128 + 2 * cap if deep else 128 + cap
     v = pltpu.VMEM
     shapes = dict(
         first=v((members, blocks * 256, 256), BF16),
         recur=v((3, blocks * 256, 256), BF16),
-        second=v((members, 128, blocks * 256), BF16),
+        second=v((members * 128, blocks * 256), BF16),
         pack=v((groups * PAIR, 128), BF16),
         unpack=v((128, groups * PAIR), BF16),
         choose=v((cap, groups * PAIR), BF16),
@@ -630,13 +725,13 @@
         factor=v((steps, 4, 256, 128), F32),
         bound=v((steps, 128, 128), F32),
         grad=v((256, 128), F32),
-        pre=v((3, 256, 128), BF16),
+        pre=v((768, 128), BF16),
         act_own=v((steps, 2, 128, 128), BF16),
         act_in=v((steps, 2, 3, 128, 128), BF16),
         policy_out=v((steps, groups, PAIR, 128), BF16),
         policy_in=v((steps, groups, PAIR, 128), BF16),
         policy=v((cap, members * 128), BF16),
-        latent=v((members, 256, cap), BF16),
+        latent=v((members * 256, cap), BF16),
         names=v((8, cap), F32),
         scaled=v((cap, blocks * 256), BF16),
         weight=v((128, 768), F32),
@@ -646,35 +741,43 @@
         back=v((cap, 256), F32),
         return_out=v((steps, groups, PAIR, 256), BF16),
         return_in=v((steps, groups, PAIR, 256), BF16),
-        held_a=v((RING, RING, 128, 128 + cap), BF16),
-        held_b=v((RING, RING, 128, 128 + cap), BF16),
-        rest_a=v((RING, 128, 128 + cap), BF16),
-        rest_b=v((RING, 128, 128 + cap), BF16),
+        held_a=v((RING, RING, 128, held), BF16),
+        held_b=v((RING, RING, 128, held), BF16),
         slope_a=v((2, RING, RING, half, 256), BF16),
         slope_b=v((2, RING, RING, half, 256), BF16),
     )
-    shapes.update(sums=[sum_bufs(128 + cap if t > 0 else 128) for t in range(steps)] + [sum_bufs(cap)])
-    copies = 4 * (groups - 1) + (steps + 1) * 24 + steps * (16 + 6 + 2 * (groups - 1))
+    if deep:
+        widths = [128] * steps + [cap] * steps
+        rests = (cap, cap, 128)
+        shapes.update(upward=v((cap, blocks * 256), F32))
+    else:
+        widths = [128] + [128 + cap] * (steps - 1) + [cap]
+        rests = (128 + cap,)
+    shapes.update(
+        sums=[sum_bufs(width) for width in widths],
+        rests=[[v((RING, 128, width), BF16) for side in range(2)] for width in rests],
+    )
+    copies = 4 * (groups - 1) + 2 * steps * 24 + steps * (16 + 6 + 2 * (groups - 1))
     shapes.update(send_sems=pltpu.SemaphoreType.DMA((copies,)))
     shapes.update(recv_sems=pltpu.SemaphoreType.DMA((copies,)))
     shapes.update(load_sems=pltpu.SemaphoreType.DMA((3,)))
     return shapes
 
 
-def call(cap, groups, blocks, name, collective_id):
+def call(cap, deep, groups, blocks, name, collective_id):
     def run(states, gates, actions, final_grad, act_w, opp_row, opp_col, recur, first, second):
         steps, members = states.shape[0], first.shape[0]
         vmem = pl.BlockSpec(memory_space=pltpu.VMEM)
         hbm = pl.BlockSpec(memory_space=pl.ANY)
         return pl.pallas_call(
-            functools.partial(kernel, steps, cap, groups, members, blocks),
+            functools.partial(kernel, steps, cap, deep, groups, members, blocks),
             out_shape=(
                 jax.ShapeDtypeStruct((256, 128), BF16),
-                jax.ShapeDtypeStruct((128, 768), F32),
+                jax.ShapeDtypeStruct((3, 128, 256), F32),
             ),
             in_specs=[vmem] * 7 + [hbm] * 3,
             out_specs=(vmem, vmem),
-            scratch_shapes=jax.tree.leaves(scratch_shapes(steps, cap, groups, members, blocks)),
+            scratch_shapes=jax.tree.leaves(scratch_shapes(steps, cap, deep, groups, members, blocks)),
             compiler_params=pltpu.CompilerParams(
                 collective_id=collective_id, has_side_effects=True, vmem_limit_bytes=62 << 20
             ),
@@ -697,10 +800,9 @@
 ):
     groups = lax.axis_size("pop")
     blocks = lax.axis_size("unit")
-    cap = groups * PAIR
     recur = jnp.transpose(recur_weight, (1, 0, 2))
     act_w = jnp.transpose(act_weight, (1, 0, 2))
-    start, weight = call(cap, groups, blocks, "steps_back", 0)(
+    operands = (
         states,
         gate_inputs,
         actions,
@@ -710,9 +812,18 @@
         opponent,
         recur,
         opp_first,
-        opp_second,
+        opp_second.reshape(-1, opp_second.shape[2]),
     )
-    return start, weight.reshape(act_weight.shape)
+    everyone = lax.all_gather(opponent[:, 0], "pop").reshape(1, -1)
+    named = everyone // opp_first.shape[0] == jnp.arange(groups, dtype=jnp.int32)[:, None]
+    most = jnp.max(jnp.sum(named.astype(jnp.int32), axis=1))
+    start, weight = lax.cond(
+        most <= FEW,
+        call(FEW, True, groups, blocks, "few_slots", 0),
+        call(groups * PAIR, False, groups, blocks, "all_slots", 1),
+        *operands,
+    )
+    return start, jnp.transpose(weight, (1, 0, 2))
 
 
 def solution(mesh):

time: 264 us -> 180 us (0.68)
  Pallas kernels: 258 us -> 163 us
  blocking collectives: 0 us -> 12 us
    pallas_call x1, Pallas kernels: 258 us -> 163 us  [run(): pl.pallas_call(functools.partial(kernel, steps, cap, deep, groups, member...]
    all_gather x0 -> x1, blocking collectives: none -> 12 us  [body(): everyone = lax.all_gather(opponent[:, 0], 'pop').reshape(1, -1)]
where the time goes in v2:
time: 180 us
  Pallas kernels  163 us (91%)
  blocking collectives  12 us (7%)
  local copies, waits for them, and re-layouts  2.77 us (2%)
    pallas_call x1, Pallas kernels, run(): pl.pallas_call(functools.partial(kernel, steps, cap, deep, groups, member...  163 us
    all_gather x1, blocking collectives, body(): everyone = lax.all_gather(opponent[:, 0], 'pop').reshape(1, -1)  12 us

profile of v2, /device:TPU:1, one launch (start us, length us, event | category | flops | bytes accessed | tf_op | source)
XLA Modules:
  0.0 180.3 jit_solution(2573162393226756828)
XLA Ops:
  0.6 12.0 %all-gather = s32[1024,1]{0,1:T(1,128)S(1)} all-gather(s32[128,1]{0,1:T(1,128)} %param.19), channel_id=2, replica_groups=mesh['pop'=8,'unit'=16] {'pop'}, dimensions={0}, use_global_device_ids=true | all-gather | bytes 4608 | tf_op jit(solution)/shard_map/all_gather | solution.py:817
  12.6 0.1 convert_reduce_fusion
  12.7 0.6 reduce_max.9
  14.0 164.9 %conditional.1 = ((bf16[256,128]{1,0:T(8,128)(2,1)S(1)}, f32[3,128,256]{2,1,0:T(8,128)S(1)})) conditional(s32[]{:T(128)} %convert_element_type.7, (bf16[4,256,128]{2,1,0:T(8,128)(2,1)}, bf16[4,3,256,128]{3,2,1,0:T(8,128)(2,1)}, bf16[4,128,128]{2,1,0:T(8,128)(2,1)}, bf16[256,128]{1,0:T(8,128)(2,1)}, bf16[3,128,256]{2,1,0:T(8,128)(2,1)}, ...), branch_computations={%region_2.3_spmd, %region_3.4_spmd} | conditional | bytes 1032 | solution.py:820
  14.3 1.4 copy.14.opp_col
  15.7 162.9 %few_slots.1 = (bf16[256,128]{1,0:T(8,128)(2,1)S(1)}, f32[3,128,256]{2,1,0:T(8,128)S(1)}) custom-call(bf16[4,256,128]{2,1,0:T(8,128)(2,1)} %get-tuple-element.50.states, bf16[4,3,256,128]{3,2,1,0:T(8,128)(2,1)} %get-tuple-element.51.gates, bf16[4,128,128]{2,1,0:T(8,128)(2,1)} %get-tuple-element.52.actions, bf16[256,128]{1,0:T(8,128)(2,1)} %get-tuple-element.53.final_grad, ...), custom_call_target="tpu_custom_call" | custom-call | tf_op jit(solution)/shard_map/cond/branch_1_fun/few_slots/pallas_call | solution.py:772
  178.9 0.6 copy.21
  179.5 0.7 copy.22
  (1 shorter events, 0.0 us)

commit v3 on v2

--- a/solution.py
+++ b/solution.py
@@ -216,6 +216,99 @@
         wait_sends(self.a1 + self.a2 + self.a3 + self.a4)
 
 
+def pair_slots(chosen, groups, members):
+    rows = chosen.shape[1]
+    group_of = (chosen // members).astype(F32)
+    index = lax.broadcasted_iota(jnp.int32, (groups, rows), 0).astype(F32)
+    onehot = jnp.where(group_of == index, 1.0, 0.0)
+    a = lax.broadcasted_iota(jnp.int32, (rows, rows), 0)
+    b = lax.broadcasted_iota(jnp.int32, (rows, rows), 1)
+    rank = mm(onehot.astype(BF16), jnp.where(a < b, 1.0, 0.0).astype(BF16))
+    key = jnp.sum(onehot * (rank + index * PAIR), axis=0, keepdims=True)
+    slot = lax.broadcasted_iota(jnp.int32, (groups * PAIR, rows), 0).astype(F32)
+    return jnp.where(slot == key, 1.0, 0.0)
+
+
+def to_groups(wire, groups, peers, p, source, target):
+    sent = [
+        wire.send(source.at[(p + k) % groups], target.at[p], device)
+        for k, device in zip(range(1, groups), peers)
+    ]
+    target[p] = source[p]
+    return sent
+
+
+def from_groups(wire, groups, p, sent, target):
+    for k, entry in zip(range(1, groups), sent):
+        wire.arrived(entry, target.at[(p + groups - k) % groups])
+
+
+def spread_kernel(
+    steps,
+    groups,
+    members,
+    states,
+    opp_row,
+    late,
+    everyone,
+    pack,
+    out_late,
+    named,
+    send_sems,
+    recv_sems,
+):
+    p = lax.axis_index("pop")
+    u = lax.axis_index("unit")
+    peers = [((p + k) % groups, u) for k in range(1, groups)]
+    barrier = pltpu.get_barrier_semaphore()
+    for device in peers:
+        pl.semaphore_signal(barrier, inc=1, device_id=device, device_id_type=MESH)
+    wire = Wire(send_sems, recv_sems)
+    named[...] = jnp.broadcast_to(opp_row[...], named.shape)
+    pack[...] = pair_slots(opp_row[...], groups, members).astype(BF16)
+    ident = jnp.broadcast_to((opp_row[...] % members + 1).astype(F32), (128, 128)).astype(BF16)
+    ident = mm_nt(pack[...], ident).astype(BF16)
+    last = steps - 1
+    packed = mm_nt(pack[...], states[last]).astype(BF16)
+    for g in range(groups):
+        out_late[g, :, 0:256] = packed[g * PAIR : (g + 1) * PAIR]
+        out_late[g, :, 256:384] = ident[g * PAIR : (g + 1) * PAIR]
+    pl.semaphore_wait(barrier, len(peers))
+    names = [wire.send(named, everyone.at[p], device) for device in peers]
+    everyone[p] = named[...]
+    lates = to_groups(wire, groups, peers, p, out_late, late)
+    from_groups(wire, groups, p, names, everyone)
+    from_groups(wire, groups, p, lates, late)
+    wait_sends(names + lates)
+
+
+def spread(states, opp_row, groups, members):
+    steps = states.shape[0]
+    vmem = pl.BlockSpec(memory_space=pltpu.VMEM)
+    shape = (groups, PAIR, 384)
+    copies = 2 * (groups - 1)
+    return pl.pallas_call(
+        functools.partial(spread_kernel, steps, groups, members),
+        out_shape=[
+            jax.ShapeDtypeStruct(shape, BF16),
+            jax.ShapeDtypeStruct((groups, 8, 128), jnp.int32),
+        ],
+        in_specs=[vmem] * 2,
+        out_specs=[vmem] * 2,
+        scratch_shapes=[
+            pltpu.VMEM((groups * PAIR, 128), BF16),
+            pltpu.VMEM(shape, BF16),
+            pltpu.VMEM((8, 128), jnp.int32),
+            pltpu.SemaphoreType.DMA((copies,)),
+            pltpu.SemaphoreType.DMA((copies,)),
+        ],
+        compiler_params=pltpu.CompilerParams(
+            collective_id=2, has_side_effects=True, vmem_limit_bytes=16 << 20
+        ),
+        name="spread",
+    )(states, opp_row)
+
+
 def kernel(
     steps,
     cap,
@@ -229,7 +322,7 @@
     final_grad,
     act_w,
     opp_row,
-    opp_col,
+    in_late,
     recur_hbm,
     first_hbm,
     second_hbm,
@@ -268,48 +361,18 @@
         load.start()
     wire = Wire(s.send_sems, s.recv_sems)
 
-    def keys(chosen, axis):
-        shape = (8, rows) if axis == 1 else (rows, 8)
-        group_of = (chosen // members).astype(F32)
-        index = lax.broadcasted_iota(jnp.int32, shape, 1 - axis).astype(F32)
-        onehot = jnp.where(group_of == index, 1.0, 0.0)
-        a = lax.broadcasted_iota(jnp.int32, (rows, rows), 0)
-        b = lax.broadcasted_iota(jnp.int32, (rows, rows), 1)
-        if axis == 1:
-            rank = mm(onehot.astype(BF16), jnp.where(a < b, 1.0, 0.0).astype(BF16))
-        else:
-            rank = mm(jnp.where(b < a, 1.0, 0.0).astype(BF16), onehot.astype(BF16))
-        return jnp.sum(onehot * (rank + index * PAIR), axis=1 - axis, keepdims=True)
-
-    key_row = keys(opp_row[...], 1)
-    key_col = keys(opp_col[...], 0)
-    slot = lax.broadcasted_iota(jnp.int32, (pair_rows, rows), 0).astype(F32)
-    s.pack[...] = jnp.where(slot == key_row, 1.0, 0.0).astype(BF16)
-    slot = lax.broadcasted_iota(jnp.int32, (rows, pair_rows), 1).astype(F32)
-    s.unpack[...] = jnp.where(slot == key_col, 1.0, 0.0).astype(BF16)
-    ident = (opp_col[...] % members + 1).astype(F32)
-    ident = jnp.broadcast_to(ident, (rows, 128)).astype(BF16)
-    ident = mm(s.pack[...], ident).astype(BF16)
-    packed = mm_nt(s.pack[...], states[last]).astype(BF16)
-    for g in range(groups):
-        s.out_late[g, :, 0:256] = packed[g * PAIR : (g + 1) * PAIR]
-        s.out_late[g, :, 256:384] = ident[g * PAIR : (g + 1) * PAIR]
+    pack = pair_slots(opp_row[...], groups, members)
+    s.pack[...] = pack.astype(BF16)
+    s.unpack[...] = pack.T.astype(BF16)
 
     pl.semaphore_wait(barrier, len(z_peers + y_peers + pop_peers))
 
     def exchange(source, target):
-        sent = [
-            wire.send(source.at[(p + k) % groups], target.at[p], device)
-            for k, device in zip(range(1, groups), pop_peers)
-        ]
-        target[p] = source[p]
-        return sent
+        return to_groups(wire, groups, pop_peers, p, source, target)
 
     def exchanged(sent, target):
-        for k, entry in zip(range(1, groups), sent):
-            wire.arrived(entry, target.at[(p + groups - k) % groups])
-
-    late = exchange(s.out_late, s.in_late)
+        from_groups(wire, groups, p, sent, target)
+
     for t in range(last):
         packed = mm_nt(s.pack[...], states[t]).astype(BF16)
         for g in range(groups):
@@ -396,7 +459,7 @@
 
     def latents(t):
         if t == last:
-            arrived = s.in_late[:, :, 0:256].reshape(pair_rows, 256)
+            arrived = in_late[:, :, 0:256].reshape(pair_rows, 256)
         else:
             arrived = s.in_early[:, t].reshape(pair_rows, 256)
         chosen = mm(s.choose[...], arrived).T
@@ -482,8 +545,7 @@
     sends = []
     act = begin(last)
 
-    exchanged(late, s.in_late)
-    names_in = s.in_late[:, :, 256:384].reshape(pair_rows, 128)
+    names_in = in_late[:, :, 256:384].reshape(pair_rows, 128)
     lane = lax.broadcasted_iota(jnp.int32, (8, 128), 1)
     picker = jnp.where(lane == 0, 1.0, 0.0).astype(BF16)
     names_row = mm_nt(picker, names_in)
@@ -580,7 +642,7 @@
         stage(later, 0, 1)
         stage(gather, 5)
         stage(following, 2)
-        sends += act + act2 + late + early + out
+        sends += act + act2 + out + early
         back = backward(last, True)
         stage(later, 2)
         stage(following, 3)
@@ -642,20 +704,20 @@
         stage(opening, 3)
         for t in range(last):
             factors(t)
-        exchanged(early, s.in_early)
         stage(opening, 4)
         loads[2].wait()
         collect(last, out)
         stage(opening, 5)
         gather = slopes(last, opening, 0)
         stage(gather, 1)
+        exchanged(early, s.in_early)
         hidden_part(last - 1, 128)
         pair = scatters(s.sums[last], s.rests[0], 0, 128 + cap)
         stage(pair, 0)
         for number in range(1, 5):
             stage(pair, number)
             stage(gather, number + 1)
-        sends += act + act2 + late + early + out
+        sends += act + act2 + out + early
         for t in range(last, -1, -1):
             if t < last:
                 act = begin(t)
@@ -713,15 +775,13 @@
         first=v((members, blocks * 256, 256), BF16),
         recur=v((3, blocks * 256, 256), BF16),
         second=v((members * 128, blocks * 256), BF16),
+        out_early=v((groups, steps - 1, PAIR, 256), BF16),
+        in_early=v((groups, steps - 1, PAIR, 256), BF16),
         pack=v((groups * PAIR, 128), BF16),
         unpack=v((128, groups * PAIR), BF16),
         choose=v((cap, groups * PAIR), BF16),
         spread=v((groups * PAIR, cap), BF16),
         mask=v((members, cap, 256), BF16),
-        out_late=v((groups, PAIR, 384), BF16),
-        in_late=v((groups, PAIR, 384), BF16),
-        out_early=v((groups, steps - 1, PAIR, 256), BF16),
-        in_early=v((groups, steps - 1, PAIR, 256), BF16),
         factor=v((steps, 4, 256, 128), F32),
         bound=v((steps, 128, 128), F32),
         grad=v((256, 128), F32),
@@ -757,7 +817,7 @@
         sums=[sum_bufs(width) for width in widths],
         rests=[[v((RING, 128, width), BF16) for side in range(2)] for width in rests],
     )
-    copies = 4 * (groups - 1) + 2 * steps * 24 + steps * (16 + 6 + 2 * (groups - 1))
+    copies = 3 * (groups - 1) + 2 * steps * 24 + steps * (16 + 6 + 2 * (groups - 1))
     shapes.update(send_sems=pltpu.SemaphoreType.DMA((copies,)))
     shapes.update(recv_sems=pltpu.SemaphoreType.DMA((copies,)))
     shapes.update(load_sems=pltpu.SemaphoreType.DMA((3,)))
@@ -765,7 +825,7 @@
 
 
 def call(cap, deep, groups, blocks, name, collective_id):
-    def run(states, gates, actions, final_grad, act_w, opp_row, opp_col, recur, first, second):
+    def run(states, gates, actions, final_grad, act_w, opp_row, late, recur, first, second):
         steps, members = states.shape[0], first.shape[0]
         vmem = pl.BlockSpec(memory_space=pltpu.VMEM)
         hbm = pl.BlockSpec(memory_space=pl.ANY)
@@ -782,7 +842,7 @@
                 collective_id=collective_id, has_side_effects=True, vmem_limit_bytes=62 << 20
             ),
             name=name,
-        )(states, gates, actions, final_grad, act_w, opp_row, opp_col, recur, first, second)
+        )(states, gates, actions, final_grad, act_w, opp_row, late, recur, first, second)
 
     return run
 
@@ -802,19 +862,21 @@
     blocks = lax.axis_size("unit")
     recur = jnp.transpose(recur_weight, (1, 0, 2))
     act_w = jnp.transpose(act_weight, (1, 0, 2))
+    opp_row = opponent.reshape(1, -1)
+    late, everyone = spread(states, opp_row, groups, opp_first.shape[0])
     operands = (
         states,
         gate_inputs,
         actions,
         final_grad,
         act_w,
-        opponent.reshape(1, -1),
-        opponent,
+        opp_row,
+        late,
         recur,
         opp_first,
         opp_second.reshape(-1, opp_second.shape[2]),
     )
-    everyone = lax.all_gather(opponent[:, 0], "pop").reshape(1, -1)
+    everyone = everyone[:, 0, :].reshape(1, -1)
     named = everyone // opp_first.shape[0] == jnp.arange(groups, dtype=jnp.int32)[:, None]
     most = jnp.max(jnp.sum(named.astype(jnp.int32), axis=1))
     start, weight = lax.cond(

time: 180 us -> 174 us (0.967)
  blocking collectives: 12 us -> 0 us
  Pallas kernels: 163 us -> 170 us
    all_gather x1 -> x0, blocking collectives: 12 us -> none  [body(): everyone = lax.all_gather(opponent[:, 0], 'pop').reshape(1, -1)]
    pallas_call x0 -> x1, Pallas kernels: none -> 10.8 us  [spread(): pl.pallas_call(functools.partial(spread_kernel, steps, groups, members),...]
    pallas_call x1, Pallas kernels: 163 us -> 159 us  [run(): pl.pallas_call(functools.partial(kernel, steps, cap, deep, groups, member...]
where the time goes in v3:
time: 174 us
  Pallas kernels  170 us (98%)
    pallas_call x1, Pallas kernels, run(): pl.pallas_call(functools.partial(kernel, steps, cap, deep, groups, member...  159 us
    pallas_call x1, Pallas kernels, spread(): pl.pallas_call(functools.partial(spread_kernel, steps, groups, members),...  10.8 us

profile of v3, /device:TPU:1, one launch (start us, length us, event | category | flops | bytes accessed | tf_op | source)
XLA Modules:
  0.0 173.7 jit_solution(5024585164105409799)
XLA Ops:
  0.6 10.8 %spread.1 = (bf16[8,48,384]{2,1,0:T(8,128)(2,1)S(1)}, s32[8,8,128]{2,1,0:T(8,128)S(1)}) custom-call(bf16[4,256,128]{2,1,0:T(8,128)(2,1)} %states.1, s32[1,128]{1,0:T(1,128)} %bitcast.14), custom_call_target="tpu_custom_call" | custom-call | tf_op jit(solution)/shard_map/spread/pallas_call | solution.py:290
  11.5 0.1 convert_reduce_fusion
  11.6 0.6 reduce_max.9
  12.9 159.4 %conditional.1 = ((bf16[256,128]{1,0:T(8,128)(2,1)S(1)}, f32[3,128,256]{2,1,0:T(8,128)S(1)})) conditional(s32[]{:T(128)} %convert_element_type.7, (bf16[4,256,128]{2,1,0:T(8,128)(2,1)}, bf16[4,3,256,128]{3,2,1,0:T(8,128)(2,1)}, bf16[4,128,128]{2,1,0:T(8,128)(2,1)}, bf16[256,128]{1,0:T(8,128)(2,1)}, bf16[3,128,256]{2,1,0:T(8,128)(2,1)}, ...), branch_computations={%region_2.3_spmd, %region_3.4_spmd} | conditional | bytes 8 | solution.py:882
  13.2 158.9 %few_slots.1 = (bf16[256,128]{1,0:T(8,128)(2,1)S(1)}, f32[3,128,256]{2,1,0:T(8,128)S(1)}) custom-call(bf16[4,256,128]{2,1,0:T(8,128)(2,1)} %get-tuple-element.50.states, bf16[4,3,256,128]{3,2,1,0:T(8,128)(2,1)} %get-tuple-element.51.gates, bf16[4,128,128]{2,1,0:T(8,128)(2,1)} %get-tuple-element.52.actions, bf16[256,128]{1,0:T(8,128)(2,1)} %get-tuple-element.53.final_grad, ...), custom_call_target="tpu_custom_call" | custom-call | tf_op jit(solution)/shard_map/cond/branch_1_fun/few_slots/pallas_call | solution.py:832
  172.4 0.6 copy.17
  173.0 0.7 copy.18
  (2 shorter events, 0.0 us)
